TPU v7x, 256 devices: a whole 4x4x8 slice. The times are simulated.
256 devices in a mesh: fsdp: 32 (over y_hi, z, core), grp: 8 (over y_lo, x).
Axes of the slice: x: 4, y: 4 (y_hi: 2, y_lo: 2; y = y_hi * 2 + y_lo), z: 8, core: 2. Of those that a mesh axis runs over, the one named last changes fastest.
Arguments:
- hidden_act: bfloat16 [8, 2048, 14336], P('grp', None, 'fsdp'), may hold values from -6 to 6
- grad_output: bfloat16 [8, 2048, 4096], P('grp', 'fsdp'), may hold values from -6 to 6
- down_weight: bfloat16 [14336, 4096], P('fsdp'), may hold values from -0.09375 to 0.09375
- proj_in: bfloat16 [14336, 64], P('fsdp'), may hold values from -0.046875 to 0.046875
- proj_out: bfloat16 [4096, 64], replicated, may hold values from -0.09375 to 0.09375
- example_ids: int32 [8, 2048], P('grp'), may hold values from 0 to 7, never falling along the last dimension, each value on 1 to 512 neighbouring positions
Outputs:
- grad_hidden: bfloat16 [8, 2048, 14336], P('grp', None, 'fsdp')
- gram: float32 [4096, 4096], P('grp', 'fsdp')
- scores: float32 [64], replicated
Inputs may be any that keep to these rules, and one draw needn't show every extreme that they name: `example_ids`: never falls along a group's tokens; each of the 8 examples of a group has 1 to 512 tokens, one exactly 512.
All inputs are finite; a program needn't handle non-finite values.
Results may differ from a plain program's by a relative error of at most 0.001.
Values may be sent and summed in bfloat16 or wider, within the bound.
No kernel may reach another device: no remote copies, remote signals or barrier semaphores. Data moves between devices by JAX's collectives and lax.ppermute only.
A program may use at most 128 MiB of HBM per device.

v0:
```python
import jax
import jax.numpy as jnp
from jax import lax
from jax.sharding import PartitionSpec as P

PROJ = 64
TOK_GRP = 2048
EX_GRP = 8


def inverse_diagonal(matrix):
    lower = jnp.linalg.cholesky(matrix)
    eye = jnp.eye(matrix.shape[0], dtype=matrix.dtype)
    lower_inv = jax.scipy.linalg.solve_triangular(lower, eye, lower=True)
    return jnp.sum(lower_inv * lower_inv, axis=0)


def example_features(ids, left, right):
    onehot = (jnp.arange(EX_GRP, dtype=jnp.int32)[:, None] == ids[None, :]).astype(jnp.float32)
    weighted = (onehot[:, None, :] * jnp.transpose(left)[None, :, :]).reshape(
        EX_GRP * PROJ, ids.shape[0]
    )
    product = jnp.dot(weighted, right, precision=lax.Precision.HIGHEST)
    return product.reshape(EX_GRP, PROJ * PROJ) * (EX_GRP / TOK_GRP) ** 0.5


def body(hidden_act, grad_output, down_weight, proj_in, proj_out, example_ids):
    fsdp_count = lax.axis_size("fsdp")
    group_count = lax.axis_size("grp")
    hidden_rows = hidden_act[0]
    grad_rows = grad_output[0]
    group_ids = example_ids[0]
    tok_rows = grad_rows.shape[0]
    feat_width = PROJ * PROJ
    examples = EX_GRP * group_count
    grad_full = lax.all_gather(grad_rows, "fsdp", axis=0, tiled=True)
    grad_hidden = lax.dot_general(
        grad_full, down_weight, (((1,), (1,)), ((), ())), preferred_element_type=jnp.float32
    )
    grad_hidden = grad_hidden.astype(jnp.bfloat16)[None]
    rows_part = hidden_rows
    left = lax.psum_scatter(
        jnp.dot(rows_part, proj_in, preferred_element_type=jnp.float32),
        "fsdp",
        scatter_dimension=0,
        tiled=True,
    )
    right = jnp.dot(grad_rows, proj_out, preferred_element_type=jnp.float32)
    my_ids = lax.dynamic_slice_in_dim(group_ids, lax.axis_index("fsdp") * tok_rows, tok_rows, 0)
    partial_feats = example_features(my_ids, left, right)
    col_count = feat_width // fsdp_count
    group_feats = lax.psum(partial_feats, "fsdp")
    all_feats = lax.all_gather(group_feats.astype(jnp.bfloat16), "grp", axis=0, tiled=True).astype(
        group_feats.dtype
    )
    own_cols = lax.dynamic_slice_in_dim(
        group_feats, lax.axis_index("fsdp") * col_count, col_count, 1
    )
    rows_part = group_feats
    product = lax.dot_general(
        rows_part,
        own_cols,
        (((0,), (0,)), ((), ())),
        precision=lax.Precision.HIGHEST,
        preferred_element_type=jnp.float32,
    )
    gram = lax.psum_scatter(product / examples, "grp", scatter_dimension=0, tiled=True)
    kernel = lax.dot_general(
        all_feats,
        all_feats,
        (((1,), (1,)), ((), ())),
        precision=lax.Precision.HIGHEST,
        preferred_element_type=jnp.float32,
    )
    ridge = jnp.trace(kernel) / examples
    eye = jnp.eye(examples, dtype=jnp.float32)
    scores = 1.0 - ridge * inverse_diagonal(kernel + ridge * eye)
    return (grad_hidden, gram, scores)


def solution(mesh):
    in_specs = (
        P("grp", None, "fsdp"),
        P("grp", "fsdp", None),
        P("fsdp", None),
        P("fsdp", None),
        P(),
        P("grp", None),
    )
    out_specs = (P("grp", None, "fsdp"), P("grp", "fsdp"), P())
    return jax.shard_map(body, mesh=mesh, in_specs=in_specs, out_specs=out_specs, check_vma=False)
```

profile of v0, /device:TPU:1, one launch (start us, length us, event | category | flops | bytes accessed | tf_op | source)
XLA Modules:
  0.0 562.3 jit_solution(12416813345016848578)
XLA Ops:
  7.2 0.0 copy-start
  7.2 0.0 copy-start.1
  7.2 0.0 copy-start.3
  7.2 0.0 reduce-scatter.3.cloned.1.call-start
  7.2 1.4 copy-done
  8.7 2.6 fusion.8
  11.3 0.0 reduce-scatter.3.cloned.1.call-update
  11.3 0.0 all-reduce.2.cloned.1.call-start
  11.3 0.7 dynamic-slice_bitcast_fusion
  12.1 0.0 copy-done.1
  12.1 0.0 copy-done.3
  12.1 0.3 fusion.11
  12.4 114.1 %reduce-scatter.3.cloned.1.call-done = f32[64,64]{1,0:T(8,128)} async-done(((f32[2048,64]{1,0:T(8,128)}), f32[64,64]{1,0:T(8,128)}) %reduce-scatter.3.cloned.1.call-update) | async-done | bytes 16400 | tf_op jit(solution)/shard_map/reduce_scatter | solution.py:42
  126.4 0.8 copy.11
  127.3 0.4 convolution_multiply_fusion.1
  127.7 0.1 copy.12
  127.9 0.8 mul.56
  128.6 0.0 all-reduce.2.cloned.1.call-update
  128.7 0.0 all-gather.3.cloned.1.call-start
  128.7 0.7 all-gather.3.cloned.1.call-update
  129.4 0.0 reduce-scatter.5.cloned.1.call-start
  129.4 246.4 %all-reduce.2.cloned.1.call-done = f32[8,4096]{1,0:T(8,128)} async-done(((f32[8,4096]{1,0:T(8,128)}), f32[8,4096]{1,0:T(8,128)}) %all-reduce.2.cloned.1.call-update) | async-done | bytes 131088 | tf_op jit(solution)/shard_map/psum | solution.py:52
  375.8 0.0 copy-start.2
  375.8 5.8 %convolution_multiply_fusion = f32[4096,128]{1,0:T(8,128)} fusion(f32[8,4096]{1,0:T(8,128)} %all-reduce.2.cloned.1.call-done, s32[]{:T(128)S(6)} %select_n.16), kind=kOutput, calls=%fused_computation.2 | convolution fusion | flops 50855936 | bytes 2232324 | tf_op jit(solution)/shard_map/dot_general | solution.py:60
  381.6 0.0 reduce-scatter.5.cloned.1.call-update
  381.6 0.0 copy-done.2
  381.7 23.1 %all_gather.7 = bf16[64,4096]{1,0:T(8,128)(2,1)S(1)} all-gather(bf16[8,4096]{1,0:T(8,128)(2,1)S(1)} %convert_element_type.18), channel_id=1, replica_groups=mesh['fsdp'=32,'grp'=8] {'grp'}, dimensions={0}, use_global_device_ids=true | all-gather | bytes 589824 | tf_op jit(solution)/shard_map/all_gather | solution.py:53
  404.7 0.9 select_reduce_fusion.1
  405.6 0.1 copy.13
  406.4 5.8 %cholesky.13 = f32[64,64]{1,0:T(8,128)S(1)} custom-call(f32[64,64]{1,0:T(8,128)S(1)} %fusion.16), custom_call_target="Cholesky" | custom-call | tf_op jit(solution)/shard_map/jit(cholesky)/cholesky | solution.py:12
  412.3 0.6 compare_reduce_fusion
  412.9 0.7 fusion.13
  413.6 4.9 custom-call.7
  418.5 0.2 fusion.10
  418.7 0.5 multiply_subtract_fusion
  419.2 97.0 %all-gather.3.cloned.1.call-done = bf16[1,2048,4096]{2,1,0:T(8,128)(2,1)} async-done(((bf16[1,64,4096]{2,1,0:T(8,128)(2,1)}), bf16[1,2048,4096]{2,1,0:T(8,128)(2,1)}) %all-gather.3.cloned.1.call-update) | async-done | bytes 16777232 | tf_op jit(solution)/shard_map/all_gather | solution.py:36
  516.3 13.3 %fusion.5 = bf16[1,2048,448]{1,2,0:T(8,128)(2,1)} fusion(bf16[448,4096]{1,0:T(8,128)(2,1)} %param.8, bf16[1,2048,4096]{2,1,0:T(8,128)(2,1)} %all-gather.3.cloned.1.call-done), kind=kOutput, calls=%fused_computation.4 | convolution fusion | flops 7517110272 | bytes 22282240 | tf_op jit(solution)/shard_map/dot_general | solution.py:37
  529.6 26.2 %reduce-scatter.5.cloned.1.call-done = f32[512,128]{1,0:T(8,128)} async-done(((f32[4096,128]{1,0:T(8,128)}), f32[512,128]{1,0:T(8,128)}) %reduce-scatter.5.cloned.1.call-update) | async-done | bytes 262160 | tf_op jit(solution)/shard_map/reduce_scatter | solution.py:67
  (5 shorter events, 0.1 us)
Async XLA Ops:
  7.2 1.5 copy-start
  7.2 4.9 copy-start.1
  7.2 4.9 copy-start.3
  7.2 119.2 %reduce-scatter.3.cloned.1.call-start = ((), (), s32[]{:S(2)}) async-start(), calls=%async_computation.2 | async-start | bytes 1081344 | tf_op jit(solution)/shard_map/reduce_scatter | solution.py:42
  11.3 364.6 %all-reduce.2.cloned.1.call-start = ((), (), s32[]{:S(2)}) async-start(), calls=%async_computation.3 | async-start | bytes 262144 | tf_op jit(solution)/shard_map/psum | solution.py:52
  128.7 387.6 %all-gather.3.cloned.1.call-start = ((), (), s32[]{:S(2)}) async-start(), calls=%async_computation.5 | async-start | bytes 17301504 | tf_op jit(solution)/shard_map/all_gather | solution.py:36
  129.4 426.4 %reduce-scatter.5.cloned.1.call-start = ((), (), s32[]{:S(2)}) async-start(), calls=%async_computation.4 | async-start | bytes 2359296 | tf_op jit(solution)/shard_map/reduce_scatter | solution.py:67
  375.8 5.8 %copy-start.2 = (f32[8,4096]{1,0:T(8,128)S(1)}, f32[8,4096]{1,0:T(8,128)}, u32[]{:S(2)}) copy-start(f32[8,4096]{1,0:T(8,128)} %all-reduce.2.cloned.1.call-done) | copy-start | bytes 393220
Sparse Core Ops, SparseCore 0:
  12.7 113.7 reduce-scatter.2
  129.8 245.9 all-reduce.1
  378.6 137.6 all-gather.2
  519.3 36.4 reduce-scatter.4
where the time goes:
time: 567 us; the launch traced here: 562 us
  waiting for transfers between devices  484 us (85%)
  matrix products  23.5 us (4%)
  blocking collectives  23.1 us (4%)
  between operations  14.5 us (3%)
  other arithmetic  12.6 us (2%)
    psum x1, waiting for transfers between devices, body(): group_feats = lax.psum(partial_feats, 'fsdp')  246 us
    reduce_scatter x1, waiting for transfers between devices, body(): lax.psum_scatter(jnp.dot(rows_part, proj_in, preferred_element_type=jnp.f...  114 us
    all_gather x1, waiting for transfers between devices, body(): grad_full = lax.all_gather(grad_rows, 'fsdp', axis=0, tiled=True)  97 us
    reduce_scatter x1, waiting for transfers between devices, body(): lax.psum_scatter(product / examples, 'grp', scatter_dimension=0, tiled=True)  26.2 us
    all_gather x1, blocking collectives, body(): lax.all_gather(group_feats.astype(jnp.bfloat16), 'grp', axis=0, tiled=True)  23.1 us
    dot_general x1, matrix products, body(): lax.dot_general(grad_full, down_weight, (((1,), (1,)), ((), ())), preferr...  13.3 us
  transfers between devices with their start and end apart: 4, of which 4 were waited for; matrix products, arithmetic and copies ran while one was open for 6% of the time, Pallas kernels for 0%

commit v1 on v0

v1 whole, which is shorter than its diff:
```python
import functools

import jax
import jax.numpy as jnp
from jax import lax
from jax.experimental import pallas as pl
from jax.experimental.pallas import tpu as pltpu
from jax.sharding import PartitionSpec as P

PROJ = 64
TOK_GRP = 2048
EX_GRP = 8
LANES = 128
PLANES = 2
RING = 8
CORES = 2
CHIPS = PLANES * RING
SAME_CORE = [[chip * CORES + core for chip in range(CHIPS)] for core in range(CORES)]
HALF = PROJ // CORES
NT = (((1,), (1,)), ((), ()))
TN = (((0,), (0,)), ((), ()))
NN = (((1,), (0,)), ((), ()))
EXACT = lax.Precision.HIGHEST
VMEM = pl.BlockSpec(memory_space=pltpu.VMEM)
SMEM = pl.BlockSpec(memory_space=pltpu.SMEM)
ANY = pl.BlockSpec(memory_space=pltpu.HBM)


def device_perm(move):
    pairs = []
    for plane in range(PLANES):
        for z in range(RING):
            for core in range(CORES):
                to_plane, to_z, to_core = move(plane, z, core)
                pairs.append(
                    (
                        (plane * RING + z) * CORES + core,
                        (to_plane * RING + to_z % RING) * CORES + to_core,
                    )
                )
    return pairs


UP = device_perm(lambda plane, z, core: (plane, z + 1, core))
DOWN = device_perm(lambda plane, z, core: (plane, z - 1, core))
ACROSS = device_perm(lambda plane, z, core: (1 - plane, z, core))
SWAP = device_perm(lambda plane, z, core: (plane, z, 1 - core))


def permute(value, pairs):
    return lax.ppermute(value, "fsdp", pairs)


def call(
    kernel, name, room, out_shape, args, scratch=(), in_specs=None, out_specs=None, aliases=None
):
    return pl.pallas_call(
        kernel,
        name=name,
        out_shape=out_shape,
        in_specs=in_specs or [SMEM] + [VMEM] * (len(args) - 1),
        out_specs=out_specs
        or (VMEM if not isinstance(out_shape, tuple) else (VMEM,) * len(out_shape)),
        scratch_shapes=list(scratch),
        input_output_aliases=aliases or {},
        compiler_params=pltpu.CompilerParams(vmem_limit_bytes=room << 20),
        cost_estimate=pl.CostEstimate(flops=0, transcendentals=0, bytes_accessed=0),
    )(*args)


def in_hbm(value):
    return pltpu.with_memory_space_constraint(value, pltpu.HBM)


def f32(*shape):
    return jax.ShapeDtypeStruct(shape, jnp.float32)


def matmul_kernel(count, place_ref, weight_hbm, *refs):
    block_refs = refs[: 2 * count]
    out_ref, weight, rows, rounded, weight_sems, row_sems, out_sems = refs[-7:]
    core = place_ref[count]
    wide = 2 * LANES
    height = weight_hbm.shape[0] // 2
    weights = [
        pltpu.make_async_copy(
            weight_hbm.at[pl.ds(i * height, height)],
            weight.at[pl.ds(i * height, height)],
            weight_sems.at[i],
        )
        for i in range(2)
    ]
    for load in weights:
        load.start()
    for b in range(count):
        for side, half in enumerate((core, 1 - core)):
            start = pl.multiple_of(b * LANES + half * 64, 64)
            pltpu.make_async_copy(
                block_refs[2 * b + side], rows.at[pl.ds(start, 64)], row_sems.at[2 * b + side]
            ).start()
    for load in weights:
        load.wait()

    def store(i, b):
        column = pl.multiple_of(place_ref[2 * i + b] * LANES, LANES)
        return pltpu.make_async_copy(
            rounded.at[i, :, pl.ds(b * LANES, LANES)],
            out_ref.at[:, pl.ds(column, LANES)],
            out_sems.at[2 * i + b],
        )

    def pair(i, carry):
        start = pl.multiple_of(i * wide, wide)
        for quarter in range(4):
            pltpu.make_async_copy(
                block_refs[0], rows.at[pl.ds(start + quarter * 64, 64)], row_sems.at[4 * i + quarter]
            ).wait()
        rounded[i] = lax.dot_general(
            weight[...], rows[pl.ds(start, wide), :], NT, preferred_element_type=jnp.float32
        ).astype(jnp.bfloat16)
        for b in range(2):
            store(i, b).start()
        return carry

    lax.fori_loop(0, count // 2, pair, 0)
    for b in range(count):
        store(b // 2, b % 2).wait()


def matmul_blocks(weight, blocks, places, core, out, tokens):
    count = len(blocks)
    width, depth = weight.shape
    flat = [array for pair in blocks for array in pair]
    args = [jnp.stack([*places, core]).astype(jnp.int32), *map(in_hbm, [weight, *flat])]
    aliases = {}
    if out is not None:
        args.append(out)
        aliases = {len(args) - 1: 0}
    return call(
        functools.partial(matmul_kernel, count),
        "grad_columns",
        14,
        jax.ShapeDtypeStruct((width, tokens), jnp.bfloat16),
        args,
        [
            pltpu.VMEM((width, depth), jnp.bfloat16),
            pltpu.VMEM((count * LANES, depth), jnp.bfloat16),
            pltpu.VMEM((count // 2, width, 2 * LANES), jnp.bfloat16),
            pltpu.SemaphoreType.DMA((2,)),
            pltpu.SemaphoreType.DMA((2 * count,)),
            pltpu.SemaphoreType.DMA((count,)),
        ],
        [SMEM] + [ANY] * (len(args) - 1),
        ANY,
        aliases,
    )


def project_kernel(
    info_ref, hidden_hbm, proj_in_hbm, rows_hbm, proj_out_hbm, kept_ref, given_ref,
    hidden, proj_in, rows, proj_out, both, sems
):
    core = info_ref[0]
    parts = 4
    width = TOK_GRP // parts
    chunks = [
        pltpu.make_async_copy(
            hidden_hbm.at[:, pl.ds(i * width, width)],
            hidden.at[:, pl.ds(i * width, width)],
            sems.at[i],
        )
        for i in range(parts)
    ]
    small = [
        pltpu.make_async_copy(source, target, sems.at[parts + i])
        for i, (source, target) in enumerate(
            ((proj_in_hbm, proj_in), (rows_hbm, rows), (proj_out_hbm, proj_out))
        )
    ]
    for load in (small[0], *chunks, small[1], small[2]):
        load.start()
    small[0].wait()
    for i in range(parts):
        chunks[i].wait()
        lanes = slice(i * width, (i + 1) * width)
        both[:, lanes] = lax.dot_general(
            proj_in[...], hidden[:, lanes], NN, preferred_element_type=jnp.float32
        )
    small[1].wait()
    small[2].wait()
    right = lax.dot_general(proj_out[...], rows[...], NT, preferred_element_type=jnp.float32)
    both[:, TOK_GRP:] = jnp.concatenate([right, jnp.zeros_like(right)], axis=1)
    kept_ref[...] = both[pl.ds(pl.multiple_of(core * HALF, HALF), HALF), :]
    given_ref[...] = both[pl.ds(pl.multiple_of((1 - core) * HALF, HALF), HALF), :]


def pack_kernel(info_ref, kept_ref, taken_ref, out_ref):
    core = info_ref[0]
    for block in range(TOK_GRP // LANES):
        lanes = slice(block * LANES, (block + 1) * LANES)
        total = kept_ref[:, lanes] + taken_ref[:, lanes]
        out_ref[:, 2 * block : 2 * block + 2, :] = total.reshape(CHIPS, 2, LANES)
    kept = kept_ref[:, TOK_GRP : TOK_GRP + 64]
    taken = taken_ref[:, TOK_GRP : TOK_GRP + 64]
    right = jnp.where(
        core == 0,
        jnp.concatenate([kept, taken], axis=1),
        jnp.concatenate([taken, kept], axis=1),
    )
    out_ref[:, HALF:, :] = jnp.broadcast_to(right[None], (CHIPS, HALF, LANES))


def left_kernel(info_ref, packed_ref, out_ref):
    total = packed_ref[0, :HALF, :]
    for chip in range(1, CHIPS):
        total += packed_ref[chip, :HALF, :]
    out_ref[...] = total


def feats_kernel(info_ref, packed_ref, left_ref, other_ref, ids_ref, out_ref, weighted, right):
    core = info_ref[0]
    low = jnp.where(core == 0, left_ref[...], other_ref[...])
    high = jnp.where(core == 0, other_ref[...], left_ref[...])
    example = lax.broadcasted_iota(jnp.int32, (EX_GRP, LANES), 0)
    for block in range(TOK_GRP // LANES):
        lanes = slice(block * LANES, (block + 1) * LANES)
        mine = ids_ref[:, lanes] == example
        for column in range(4):
            source = low if column < 2 else high
            row = 2 * block + column % 2
            weighted[column * EX_GRP : (column + 1) * EX_GRP, lanes] = jnp.where(
                mine, source[row : row + 1, :], 0.0
            )
        right[:, lanes] = packed_ref[block, HALF:, :]
    sums = lax.dot_general(
        weighted[...], right[...], NT, precision=EXACT, preferred_element_type=jnp.float32
    )
    sums = sums * (EX_GRP / TOK_GRP) ** 0.5
    wide = jnp.concatenate(
        [sums[c * EX_GRP : (c + 1) * EX_GRP, :] for c in range(4)], axis=1
    )
    out_ref[...] = jnp.broadcast_to(wide[None], out_ref.shape)


def finish_kernel(examples, info_ref, mine_ref, other_ref, gram_ref, scores_ref, full):
    core, device, group = info_ref[0], info_ref[1], info_ref[2]
    for chip in range(CHIPS):
        rows = slice(chip * EX_GRP, (chip + 1) * EX_GRP)
        for part, ref in enumerate((mine_ref, other_ref)):
            start = (part * CHIPS + chip) * LANES
            full[:, start : start + LANES] = ref[:, rows, :].reshape(examples, LANES)

    def columns(chip, upper):
        start = pl.multiple_of(chip * EX_GRP, EX_GRP)
        halves = []
        for ref in (mine_ref, other_ref):
            part = ref[:, pl.ds(start, EX_GRP), :].reshape(examples, LANES)
            halves.append(jnp.where(upper == 0, part[:, :64], part[:, 64:]))
        first = jnp.where(core == 0, halves[0], halves[1])
        second = jnp.where(core == 0, halves[1], halves[0])
        return jnp.concatenate(
            [first[:, :HALF], second[:, :HALF], first[:, HALF:], second[:, HALF:]], axis=1
        )

    cols = columns(device % CHIPS, device // CHIPS)
    per_group = CHIPS // 4
    rows = jnp.concatenate(
        [columns(per_group * (group % 4) + q, group // 4) for q in range(per_group)], axis=1
    )
    gram_ref[...] = (
        lax.dot_general(rows, cols, TN, precision=EXACT, preferred_element_type=jnp.float32)
        / examples
    )
    kernel = lax.dot_general(
        full[...], full[...], NT, precision=EXACT, preferred_element_type=jnp.float32
    )
    sub = lax.broadcasted_iota(jnp.int32, kernel.shape, 0)
    lane = lax.broadcasted_iota(jnp.int32, kernel.shape, 1)
    diagonal = sub == lane
    ridge = jnp.sum(jnp.where(diagonal, kernel, 0.0)) / examples
    matrix = jnp.where(diagonal, kernel + ridge, kernel)
    for k in range(examples):
        column = matrix[:, k : k + 1]
        pivot = matrix[k : k + 1, k : k + 1]
        row = jnp.where(lane[:1] == k, 1.0, matrix[k : k + 1, :]) / pivot
        cleared = jnp.where(lane == k, 0.0, matrix) - column * row
        matrix = jnp.where(sub == k, row, cleared)
    inverse = jnp.sum(jnp.where(diagonal, matrix, 0.0), axis=0, keepdims=True)
    scores_ref[...] = 1.0 - ridge * inverse


def body(hidden_act, grad_output, down_weight, proj_in, proj_out, example_ids):
    group_count = lax.axis_size("grp")
    examples = EX_GRP * group_count
    device = lax.axis_index("fsdp")
    core = device % CORES
    plane = device // (RING * CORES)
    z = (device // CORES) % RING
    info = jnp.stack([core, device, lax.axis_index("grp")]).astype(jnp.int32)
    grad_rows = grad_output[0]
    tie = lax.optimization_barrier

    def chip(side, offset):
        return side * RING + (z + offset) % RING

    def columns(out, blocks):
        made = [((rows, permute(rows, SWAP)), chip(side, at)) for rows, side, at in blocks]
        return matmul_blocks(
            down_weight, [m[0] for m in made], [m[1] for m in made], core, out, TOK_GRP
        )

    near, away = plane, 1 - plane
    below1 = permute(grad_rows, UP)
    above1 = permute(grad_rows, DOWN)
    far0 = permute(grad_rows, ACROSS)
    hidden = jnp.transpose(hidden_act[0])
    kept, given = call(
        project_kernel,
        "project",
        10,
        (f32(HALF, TOK_GRP + LANES),) * 2,
        [
            info,
            *map(in_hbm, [hidden, jnp.transpose(proj_in), grad_rows, jnp.transpose(proj_out)]),
        ],
        [
            pltpu.VMEM(hidden.shape, jnp.bfloat16),
            pltpu.VMEM(proj_in.shape[::-1], jnp.bfloat16),
            pltpu.VMEM(grad_rows.shape, jnp.bfloat16),
            pltpu.VMEM(proj_out.shape[::-1], jnp.bfloat16),
            pltpu.VMEM((PROJ, TOK_GRP + LANES), jnp.float32),
            pltpu.SemaphoreType.DMA((7,)),
        ],
        [SMEM] + [ANY] * 4,
    )
    packed = call(
        pack_kernel, "pack", 6, f32(CHIPS, PROJ, LANES), [info, kept, permute(given, SWAP)]
    )
    below1, above1, far0, packed = tie((below1, above1, far0, packed))

    below2 = permute(below1, UP)
    above2 = permute(above1, DOWN)
    far_above1 = permute(above1, ACROSS)
    packed = lax.all_to_all(packed, "fsdp", 0, 0, axis_index_groups=SAME_CORE, tiled=True)
    out = columns(
        None, [(grad_rows, near, 0), (below1, near, -1), (above1, near, 1), (far0, away, 0)]
    )
    below2, above2, far_above1, out = tie((below2, above2, far_above1, out))

    below3 = permute(below2, UP)
    above3 = permute(above2, DOWN)
    far_below1 = permute(below1, ACROSS)
    left = call(left_kernel, "left", 4, f32(HALF, LANES), [info, packed])
    feats = call(
        feats_kernel,
        "feats",
        6,
        f32(CHIPS, EX_GRP, LANES),
        [info, packed, left, permute(left, SWAP), example_ids],
        [pltpu.VMEM((4 * EX_GRP, TOK_GRP), jnp.float32), pltpu.VMEM((HALF, TOK_GRP), jnp.float32)],
    )
    below3, above3, far_below1, feats = tie((below3, above3, far_below1, feats))

    far_below2 = permute(far_below1, UP)
    above4 = permute(above3, DOWN)
    far_above2 = permute(above2, ACROSS)
    feats = lax.all_to_all(feats, "fsdp", 0, 0, axis_index_groups=SAME_CORE, tiled=True)
    out = columns(
        out, [(below2, near, -2), (above2, near, 2), (far_above1, away, 1), (below3, near, -3)]
    )
    far_below2, above4, far_above2, out, feats = tie((far_below2, above4, far_above2, out, feats))

    far_below3 = permute(far_below2, UP)
    far_above3 = permute(far_above2, DOWN)
    far_above4 = permute(above4, ACROSS)
    feats = lax.all_to_all(
        jnp.broadcast_to(
            feats.reshape(1, CHIPS * EX_GRP, LANES), (group_count, CHIPS * EX_GRP, LANES)
        ),
        "grp",
        0,
        0,
        tiled=True,
    )
    out = columns(
        out,
        [(above3, near, 3), (far_below1, away, -1), (far_below2, away, -2), (above4, near, 4)],
    )
    far_below3, far_above3, far_above4, out, feats = tie(
        (far_below3, far_above3, far_above4, out, feats)
    )
    out = columns(
        out,
        [
            (far_above2, away, 2),
            (far_below3, away, -3),
            (far_above3, away, 3),
            (far_above4, away, 4),
        ],
    )
    gram, scores = call(
        functools.partial(finish_kernel, examples),
        "finish",
        12,
        (f32(PROJ * PROJ // group_count, LANES), f32(1, examples)),
        [info, feats, permute(feats, SWAP)],
        [pltpu.VMEM((examples, PROJ * PROJ), jnp.float32)],
    )
    return (jnp.transpose(out)[None], gram, scores[0])


def solution(mesh):
    in_specs = (
        P("grp", None, "fsdp"),
        P("grp", "fsdp", None),
        P("fsdp", None),
        P("fsdp", None),
        P(),
        P("grp", None),
    )
    out_specs = (P("grp", None, "fsdp"), P("grp", "fsdp"), P())
    return jax.shard_map(body, mesh=mesh, in_specs=in_specs, out_specs=out_specs, check_vma=False)
```

time: 567 us -> 127 us (0.22)
  waiting for transfers between devices: 484 us -> 17.9 us
  starting transfers between devices: 0.16 us -> 64.3 us
  Pallas kernels: 0 us -> 40 us
  matrix products: 23.5 us -> 0 us
  blocking collectives: 23.1 us -> 0 us
  between operations: 14.5 us -> 1.23 us
  other arithmetic: 12.6 us -> 0.08 us
    psum x1 -> x0, waiting for transfers between devices: 246 us -> none  [body(): group_feats = lax.psum(partial_feats, 'fsdp')]
    reduce_scatter x2 -> x0, waiting for transfers between devices: 140 us -> none  [the longest x1 114 us: body(): lax.psum_scatter(jnp.dot(rows_part, proj_in, preferred_element_type=jnp.f...]
    all_gather x1 -> x0, waiting for transfers between devices: 97 us -> none  [body(): grad_full = lax.all_gather(grad_rows, 'fsdp', axis=0, tiled=True)]
    ppermute x0 -> x34, starting transfers between devices: none -> 49.5 us  [permute(): return lax.ppermute(value, 'fsdp', pairs)]
    pallas_call x0 -> x9, Pallas kernels: none -> 40 us  [call(): pl.pallas_call(kernel, name=name, out_shape=out_shape, in_specs=in_specs...]
    dot_general x6 -> x0, matrix products: 23.3 us -> none  [the longest x1 13.3 us: body(): lax.dot_general(grad_full, down_weight, (((1,), (1,)), ((), ())), preferr...]
    all_gather x1 -> x0, blocking collectives: 23.1 us -> none  [body(): lax.all_gather(group_feats.astype(jnp.bfloat16), 'grp', axis=0, tiled=True)]
    all_to_all x0 -> x3, starting transfers between devices: none -> 14.7 us  [the longest x1 5.3 us: body(): lax.all_to_all(packed, 'fsdp', 0, 0, axis_index_groups=SAME_CORE, tiled=T...]
  transfers between devices with their start and end apart: 4 -> 37, of which waited for: 4 -> 9; matrix products, arithmetic and copies ran while one was open for 6% -> 1% of each run, Pallas kernels for 0% -> 27%
where the time goes in v1:
time: 127 us; the launch traced here: 126 us
  starting transfers between devices  64.3 us (51%)
  Pallas kernels  40 us (31%)
  waiting for transfers between devices  17.9 us (14%)
  local copies, waits for them, and re-layouts  3.02 us (2%)
    ppermute x34, starting transfers between devices, permute(): return lax.ppermute(value, 'fsdp', pairs)  49.5 us
    pallas_call x9, Pallas kernels, call(): pl.pallas_call(kernel, name=name, out_shape=out_shape, in_specs=in_specs...  40 us
    ppermute x34, waiting for transfers between devices, permute(): return lax.ppermute(value, 'fsdp', pairs)  7.71 us
    all_to_all x1, starting transfers between devices, body(): lax.all_to_all(packed, 'fsdp', 0, 0, axis_index_groups=SAME_CORE, tiled=T...  5.3 us
    all_to_all x1, starting transfers between devices, body(): lax.all_to_all(feats, 'fsdp', 0, 0, axis_index_groups=SAME_CORE, tiled=True)  5.3 us
    all_to_all x1, waiting for transfers between devices, body(): lax.all_to_all(jnp.broadcast_to(feats.reshape(1, CHIPS * EX_GRP, LANES),...  4.22 us
    all_to_all x1, starting transfers between devices, body(): lax.all_to_all(jnp.broadcast_to(feats.reshape(1, CHIPS * EX_GRP, LANES),...  4.13 us
    all_to_all x1, waiting for transfers between devices, body(): lax.all_to_all(packed, 'fsdp', 0, 0, axis_index_groups=SAME_CORE, tiled=T...  3.42 us
  transfers between devices with their start and end apart: 37, of which 9 were waited for; matrix products, arithmetic and copies ran while one was open for 1% of the time, Pallas kernels for 27%

profile of v1, /device:TPU:1, one launch (start us, length us, event | category | flops | bytes accessed | tf_op | source)
XLA Modules:
  0.0 126.4 jit_solution(12801139883817983994)
XLA Ops:
  0.6 2.5 %collective-permute-start = (bf16[64,4096]{1,0:T(8,128)(2,1)}, bf16[64,4096]{1,0:T(8,128)(2,1)S(1)}, u32[]{:S(2)}, u32[]{:S(2)}) collective-permute-start(bf16[64,4096]{1,0:T(8,128)(2,1)} %bitcast.31), channel_id=1, source_target_pairs={{0,16},{8,24},{16,32},{24,40},{32,48},{40,56},{48,64},{56,72},{64,... | collective-permute-start | bytes 1572872 | tf_op jit(solution)/shard_map/ppermute | solution.py:51
  3.2 4.0 %collective-permute-start.1 = (bf16[64,4096]{1,0:T(8,128)(2,1)}, bf16[64,4096]{1,0:T(8,128)(2,1)}, u32[]{:S(2)}, u32[]{:S(2)}) collective-permute-start(bf16[64,4096]{1,0:T(8,128)(2,1)} %bitcast.32), channel_id=1, source_target_pairs={{0,112},{8,120},{16,0},{24,8},{32,16},{40,24},{48,32},{56,40},{64,... | collective-permute-start | bytes 1572872 | tf_op jit(solution)/shard_map/ppermute | solution.py:51
  7.2 2.9 %collective-permute-start.2 = (bf16[64,4096]{1,0:T(8,128)(2,1)}, bf16[64,4096]{1,0:T(8,128)(2,1)S(1)}, u32[]{:S(2)}, u32[]{:S(2)}) collective-permute-start(bf16[64,4096]{1,0:T(8,128)(2,1)} %bitcast.33), channel_id=1, source_target_pairs={{0,128},{8,136},{16,144},{24,152},{32,160},{40,168},{48,176},{56,1... | collective-permute-start | bytes 1572872 | tf_op jit(solution)/shard_map/ppermute | solution.py:51
  10.2 3.1 %project.1 = (f32[32,2176]{1,0:T(8,128)S(1)}, f32[32,2176]{1,0:T(8,128)S(1)}) custom-call(s32[3]{0:T(128)S(1)} %pad_add_fusion.info_ref, bf16[448,2048]{1,0:T(8,128)(2,1)} %bitcast.37, bf16[64,448]{1,0:T(8,128)(2,1)} %bitcast.40, bf16[64,4096]{1,0:T(8,128)(2,1)} %bitcast.34, bf16[64,4096]{1,0:T(8,128)(2,1)} %bitcast.38), custom_call_target="tpu_custom_call" | custom-call | tf_op jit(solution)/shard_map/project/pallas_call | solution.py:57
  13.3 1.3 %collective-permute-start.3 = (f32[32,2176]{1,0:T(8,128)S(1)}, f32[32,2176]{1,0:T(8,128)S(1)}, u32[]{:S(2)}, u32[]{:S(2)}) collective-permute-start(f32[32,2176]{1,0:T(8,128)S(1)} %get-tuple-element.30), channel_id=1, source_target_pairs={{0,8},{8,0},{16,24},{24,16},{32,40},{40,32},{48,56},{56,48},{64,72... | collective-permute-start | bytes 835592 | tf_op jit(solution)/shard_map/ppermute | solution.py:51
  14.7 1.1 collective-permute-done.3.taken_ref
  15.8 1.5 %pack.1 = f32[16,64,128]{2,1,0:T(8,128)} custom-call(s32[3]{0:T(128)S(1)} %pad_add_fusion.info_ref, f32[32,2176]{1,0:T(8,128)S(1)} %get-tuple-element.29.kept_ref, f32[32,2176]{1,0:T(8,128)S(1)} %collective-permute-done.3.taken_ref), custom_call_target="tpu_custom_call" | custom-call | tf_op jit(solution)/shard_map/pack/pallas_call | solution.py:57
  17.3 1.7 %collective-permute-done.refs_2_ = bf16[64,4096]{1,0:T(8,128)(2,1)S(1)} collective-permute-done((bf16[64,4096]{1,0:T(8,128)(2,1)}, bf16[64,4096]{1,0:T(8,128)(2,1)S(1)}, u32[]{:S(2)}, u32[]{:S(2)}) %collective-permute-start) | collective-permute-done | bytes 524320 | tf_op jit(solution)/shard_map/ppermute | solution.py:51
  19.0 2.4 %collective-permute-done.2.refs_6_ = bf16[64,4096]{1,0:T(8,128)(2,1)S(1)} collective-permute-done((bf16[64,4096]{1,0:T(8,128)(2,1)}, bf16[64,4096]{1,0:T(8,128)(2,1)S(1)}, u32[]{:S(2)}, u32[]{:S(2)}) %collective-permute-start.2) | collective-permute-done | bytes 524320 | tf_op jit(solution)/shard_map/ppermute | solution.py:51
  21.4 1.8 %collective-permute-start.10 = (bf16[64,4096]{1,0:T(8,128)(2,1)S(1)}, bf16[64,4096]{1,0:T(8,128)(2,1)}, u32[]{:S(2)}, u32[]{:S(2)}) collective-permute-start(bf16[64,4096]{1,0:T(8,128)(2,1)S(1)} %collective-permute-done.2.refs_6_), channel_id=1, source_target_pairs={{0,8},{8,0},{16,24},{24,16},{32,40},{40,32},{48,56},{56,48},{64,72... | collective-permute-start | bytes 1572872 | tf_op jit(solution)/shard_map/ppermute | solution.py:51
  23.3 0.5 collective-permute-start.9
  23.8 2.7 %collective-permute-start.5 = (bf16[64,4096]{1,0:T(8,128)(2,1)}, bf16[64,4096]{1,0:T(8,128)(2,1)S(1)}, u32[]{:S(2)}, u32[]{:S(2)}) collective-permute-start(bf16[64,4096]{1,0:T(8,128)(2,1)} %collective-permute-done.1.refs_4_), channel_id=1, source_target_pairs={{0,112},{8,120},{16,0},{24,8},{32,16},{40,24},{48,32},{56,40},{64,... | collective-permute-start | bytes 1572872 | tf_op jit(solution)/shard_map/ppermute | solution.py:51
  26.5 2.9 %collective-permute-start.6 = (bf16[64,4096]{1,0:T(8,128)(2,1)}, bf16[64,4096]{1,0:T(8,128)(2,1)S(1)}, u32[]{:S(2)}, u32[]{:S(2)}) collective-permute-start(bf16[64,4096]{1,0:T(8,128)(2,1)} %collective-permute-done.1.refs_4_), channel_id=1, source_target_pairs={{0,128},{8,136},{16,144},{24,152},{32,160},{40,168},{48,176},{56,1... | collective-permute-start | bytes 1572872 | tf_op jit(solution)/shard_map/ppermute | solution.py:51
  29.4 5.3 %all-to-all-start = ((f32[16,64,128]{2,1,0:T(8,128)}), f32[16,64,128]{2,1,0:T(8,128)S(1)}, u32[]{:S(2)}, u32[]{:S(2)}) async-start(f32[16,64,128]{2,1,0:T(8,128)} %pack.1), calls=%async_computation | async-start | bytes 1048576 | tf_op jit(solution)/shard_map/all_to_all | solution.py:344
  34.9 2.9 %collective-permute-start.13 = (bf16[64,4096]{1,0:T(8,128)(2,1)S(1)}, bf16[64,4096]{1,0:T(8,128)(2,1)S(1)}, u32[]{:S(2)}, u32[]{:S(2)}) collective-permute-start(bf16[64,4096]{1,0:T(8,128)(2,1)S(1)} %collective-permute-done.refs_2_), channel_id=1, source_target_pairs={{0,128},{8,136},{16,144},{24,152},{32,160},{40,168},{48,176},{56,1... | collective-permute-start | bytes 1572872 | tf_op jit(solution)/shard_map/ppermute | solution.py:51
  37.7 6.3 %grad_columns.4.refs_8_ = bf16[448,2048]{1,0:T(8,128)(2,1)} custom-call(s32[5]{0:T(128)S(1)} %stack.89.place_ref, bf16[448,4096]{1,0:T(8,128)(2,1)} %weight_hbm.7, bf16[64,4096]{1,0:T(8,128)(2,1)} %bitcast.35, bf16[64,4096]{1,0:T(8,128)(2,1)} %copy-done.10, bf16[64,4096]{1,0:T(8,128)(2,1)} %copy-done.7, bf16[64,4096]{1,0:T(8,128)(2,1)} %collective-permute-done.8.refs_3_, ...), custom_call_target="tpu_custom_call" | custom-call | tf_op jit(solution)/shard_map/grad_columns/pallas_call | solution.py:57
  44.1 1.3 collective-permute-start.11
  45.4 1.5 %collective-permute-start.12 = (bf16[64,4096]{1,0:T(8,128)(2,1)S(1)}, bf16[64,4096]{1,0:T(8,128)(2,1)}, u32[]{:S(2)}, u32[]{:S(2)}) collective-permute-start(bf16[64,4096]{1,0:T(8,128)(2,1)S(1)} %collective-permute-done.5.refs_2_), channel_id=1, source_target_pairs={{0,112},{8,120},{16,0},{24,8},{32,16},{40,24},{48,32},{56,40},{64,... | collective-permute-start | bytes 1572872 | tf_op jit(solution)/shard_map/ppermute | solution.py:51
  46.9 3.4 %all-to-all-done.packed_ref = f32[16,64,128]{2,1,0:T(8,128)S(1)} async-done(((f32[16,64,128]{2,1,0:T(8,128)}), f32[16,64,128]{2,1,0:T(8,128)S(1)}, u32[]{:S(2)}, u32[]{:S(2)}) %all-to-all-start) | async-done | bytes 524320 | tf_op jit(solution)/shard_map/all_to_all | solution.py:344
  50.3 0.6 left.1.left_ref
  50.8 4.7 %collective-permute-start.14 = (f32[32,128]{1,0:T(8,128)S(1)}, f32[32,128]{1,0:T(8,128)S(1)}, u32[]{:S(2)}, u32[]{:S(2)}) collective-permute-start(f32[32,128]{1,0:T(8,128)S(1)} %left.1.left_ref), channel_id=1, source_target_pairs={{0,8},{8,0},{16,24},{24,16},{32,40},{40,32},{48,56},{56,48},{64,72... | collective-permute-start | bytes 49160 | tf_op jit(solution)/shard_map/ppermute | solution.py:51
  55.8 0.6 collective-permute-done.14.other_ref
  56.7 1.6 %feats.1 = f32[16,8,128]{2,1,0:T(8,128)} custom-call(s32[3]{0:T(128)S(1)} %pad_add_fusion.info_ref, f32[16,64,128]{2,1,0:T(8,128)S(1)} %all-to-all-done.packed_ref, f32[32,128]{1,0:T(8,128)S(1)} %left.1.left_ref, f32[32,128]{1,0:T(8,128)S(1)} %collective-permute-done.14.other_ref, s32[1,2048]{1,0:T(1,128)S(1)} %copy-done), custom_call_target="tpu_custom_call" | custom-call | tf_op jit(solution)/shard_map/feats/pallas_call | solution.py:57
  58.3 1.1 collective-permute-start.20
  59.4 1.2 collective-permute-done.11.refs_6_
  60.6 1.3 %collective-permute-start.21 = (bf16[64,4096]{1,0:T(8,128)(2,1)}, bf16[64,4096]{1,0:T(8,128)(2,1)S(1)}, u32[]{:S(2)}, u32[]{:S(2)}) collective-permute-start(bf16[64,4096]{1,0:T(8,128)(2,1)} %collective-permute-done.11.refs_6_), channel_id=1, source_target_pairs={{0,8},{8,0},{16,24},{24,16},{32,40},{40,32},{48,56},{56,48},{64,72... | collective-permute-start | bytes 1572872 | tf_op jit(solution)/shard_map/ppermute | solution.py:51
  61.9 2.9 %collective-permute-start.17 = (bf16[64,4096]{1,0:T(8,128)(2,1)S(1)}, bf16[64,4096]{1,0:T(8,128)(2,1)S(1)}, u32[]{:S(2)}, u32[]{:S(2)}) collective-permute-start(bf16[64,4096]{1,0:T(8,128)(2,1)S(1)} %collective-permute-done.5.refs_2_), channel_id=1, source_target_pairs={{0,128},{8,136},{16,144},{24,152},{32,160},{40,168},{48,176},{56,1... | collective-permute-start | bytes 1572872 | tf_op jit(solution)/shard_map/ppermute | solution.py:51
  64.9 3.0 %collective-permute-start.16 = (bf16[64,4096]{1,0:T(8,128)(2,1)}, bf16[64,4096]{1,0:T(8,128)(2,1)}, u32[]{:S(2)}, u32[]{:S(2)}) collective-permute-start(bf16[64,4096]{1,0:T(8,128)(2,1)} %collective-permute-done.12.refs_0_), channel_id=1, source_target_pairs={{0,112},{8,120},{16,0},{24,8},{32,16},{40,24},{48,32},{56,40},{64,... | collective-permute-start | bytes 1572872 | tf_op jit(solution)/shard_map/ppermute | solution.py:51
  67.8 0.6 collective-permute-start.26
  68.6 0.8 copy-done.15
  69.4 0.6 collective-permute-start.27
  70.0 5.3 %all-to-all-start.1 = ((f32[16,8,128]{2,1,0:T(8,128)}), f32[16,8,128]{2,1,0:T(8,128)S(1)}, u32[]{:S(2)}, u32[]{:S(2)}) async-start(f32[16,8,128]{2,1,0:T(8,128)} %feats.1), calls=%async_computation.1 | async-start | bytes 131072 | tf_op jit(solution)/shard_map/all_to_all | solution.py:367
  75.5 6.3 %grad_columns.5.refs_8_ = bf16[448,2048]{1,0:T(8,128)(2,1)} custom-call(s32[5]{0:T(128)S(1)} %stack.94.place_ref, bf16[448,4096]{1,0:T(8,128)(2,1)} %weight_hbm.7, bf16[64,4096]{1,0:T(8,128)(2,1)} %copy-done.3, bf16[64,4096]{1,0:T(8,128)(2,1)} %copy-done.12, bf16[64,4096]{1,0:T(8,128)(2,1)} %copy-done.2, ...), custom_call_target="tpu_custom_call", output_to_operand_aliasing={{}: (10, {})} | custom-call | tf_op jit(solution)/shard_map/grad_columns/pallas_call | solution.py:57
  81.8 2.5 %all-to-all-done.1 = f32[16,8,128]{2,1,0:T(8,128)S(1)} async-done(((f32[16,8,128]{2,1,0:T(8,128)}), f32[16,8,128]{2,1,0:T(8,128)S(1)}, u32[]{:S(2)}, u32[]{:S(2)}) %all-to-all-start.1) | async-done | bytes 65568 | tf_op jit(solution)/shard_map/all_to_all | solution.py:367
  84.3 1.4 %collective-permute-start.28 = (bf16[64,4096]{1,0:T(8,128)(2,1)S(1)}, bf16[64,4096]{1,0:T(8,128)(2,1)S(1)}, u32[]{:S(2)}, u32[]{:S(2)}) collective-permute-start(bf16[64,4096]{1,0:T(8,128)(2,1)S(1)} %collective-permute-done.15.refs_4_), channel_id=1, source_target_pairs={{0,8},{8,0},{16,24},{24,16},{32,40},{40,32},{48,56},{56,48},{64,72... | collective-permute-start | bytes 1572872 | tf_op jit(solution)/shard_map/ppermute | solution.py:51
  85.8 0.9 collective-permute-start.23
  86.7 1.8 %collective-permute-start.24 = (bf16[64,4096]{1,0:T(8,128)(2,1)S(1)}, bf16[64,4096]{1,0:T(8,128)(2,1)}, u32[]{:S(2)}, u32[]{:S(2)}) collective-permute-start(bf16[64,4096]{1,0:T(8,128)(2,1)S(1)} %collective-permute-done.17.refs_0_), channel_id=1, source_target_pairs={{0,112},{8,120},{16,0},{24,8},{32,16},{40,24},{48,32},{56,40},{64,... | collective-permute-start | bytes 1572872 | tf_op jit(solution)/shard_map/ppermute | solution.py:51
  88.5 1.8 %collective-permute-start.25 = (bf16[64,4096]{1,0:T(8,128)(2,1)}, bf16[64,4096]{1,0:T(8,128)(2,1)S(1)}, u32[]{:S(2)}, u32[]{:S(2)}) collective-permute-start(bf16[64,4096]{1,0:T(8,128)(2,1)} %collective-permute-done.16.refs_6_), channel_id=1, source_target_pairs={{0,128},{8,136},{16,144},{24,152},{32,160},{40,168},{48,176},{56,1... | collective-permute-start | bytes 1572872 | tf_op jit(solution)/shard_map/ppermute | solution.py:51
  90.3 0.8 broadcast_in_dim.11
  91.1 4.1 %all-to-all-start.2 = ((f32[8,128,128]{2,1,0:T(8,128)}), f32[8,128,128]{2,1,0:T(8,128)S(1)}, u32[]{:S(2)}, u32[]{:S(2)}) async-start(f32[8,128,128]{2,1,0:T(8,128)} %broadcast_in_dim.11), calls=%async_computation.2 | async-start | bytes 1048576 | tf_op jit(solution)/shard_map/all_to_all | solution.py:376
  95.4 1.6 %collective-permute-start.22 = (bf16[64,4096]{1,0:T(8,128)(2,1)S(1)}, bf16[64,4096]{1,0:T(8,128)(2,1)}, u32[]{:S(2)}, u32[]{:S(2)}) collective-permute-start(bf16[64,4096]{1,0:T(8,128)(2,1)S(1)} %collective-permute-done.17.refs_0_), channel_id=1, source_target_pairs={{0,8},{8,0},{16,24},{24,16},{32,40},{40,32},{48,56},{56,48},{64,72... | collective-permute-start | bytes 1572872 | tf_op jit(solution)/shard_map/ppermute | solution.py:51
  97.0 6.3 %grad_columns.6.refs_8_ = bf16[448,2048]{1,0:T(8,128)(2,1)} custom-call(s32[5]{0:T(128)S(1)} %stack.99.place_ref, bf16[448,4096]{1,0:T(8,128)(2,1)} %weight_hbm.7, bf16[64,4096]{1,0:T(8,128)(2,1)} %collective-permute-done.12.refs_0_, bf16[64,4096]{1,0:T(8,128)(2,1)} %collective-permute-done.26.refs_1_, ...), custom_call_target="tpu_custom_call", output_to_operand_aliasing={{}: (10, {})} | custom-call | tf_op jit(solution)/shard_map/grad_columns/pallas_call | solution.py:57
  103.3 4.2 %all-to-all-done.2.mine_ref = f32[8,128,128]{2,1,0:T(8,128)S(1)} async-done(((f32[8,128,128]{2,1,0:T(8,128)}), f32[8,128,128]{2,1,0:T(8,128)S(1)}, u32[]{:S(2)}, u32[]{:S(2)}) %all-to-all-start.2) | async-done | bytes 524320 | tf_op jit(solution)/shard_map/all_to_all | solution.py:376
  107.5 2.0 %collective-permute-start.33 = (f32[8,128,128]{2,1,0:T(8,128)S(1)}, f32[8,128,128]{2,1,0:T(8,128)S(1)}, u32[]{:S(2)}, u32[]{:S(2)}) collective-permute-start(f32[8,128,128]{2,1,0:T(8,128)S(1)} %all-to-all-done.2.mine_ref), channel_id=1, source_target_pairs={{0,8},{8,0},{16,24},{24,16},{32,40},{40,32},{48,56},{56,48},{64,72... | collective-permute-start | bytes 1572872 | tf_op jit(solution)/shard_map/ppermute | solution.py:51
  110.4 0.6 collective-permute-done.33.other_ref
  111.0 8.1 %finish.1 = (f32[512,128]{1,0:T(8,128)}, f32[1,64]{1,0:T(1,128)}) custom-call(s32[3]{0:T(128)S(1)} %pad_add_fusion.info_ref, f32[8,128,128]{2,1,0:T(8,128)S(1)} %all-to-all-done.2.mine_ref, f32[8,128,128]{2,1,0:T(8,128)S(1)} %collective-permute-done.33.other_ref), custom_call_target="tpu_custom_call" | custom-call | tf_op jit(solution)/shard_map/finish/pallas_call | solution.py:57
  119.2 0.8 copy-done.17
  120.0 6.3 %grad_columns.7 = bf16[448,2048]{1,0:T(8,128)(2,1)} custom-call(s32[5]{0:T(128)S(1)} %stack.81.place_ref, bf16[448,4096]{1,0:T(8,128)(2,1)} %weight_hbm.7, bf16[64,4096]{1,0:T(8,128)(2,1)} %copy-done.5, bf16[64,4096]{1,0:T(8,128)(2,1)} %collective-permute-done.22.refs_1_, ...), custom_call_target="tpu_custom_call", output_to_operand_aliasing={{}: (10, {})} | custom-call | tf_op jit(solution)/shard_map/grad_columns/pallas_call | solution.py:57
  (77 shorter events, 2.5 us)
Async XLA Ops:
  0.6 14.0 %copy-start.1 = (bf16[1,64,4096]{2,1,0:T(8,128)(2,1)S(1)}, bf16[1,64,4096]{2,1,0:T(8,128)(2,1)}, u32[]{:S(2)}) copy-start(bf16[1,64,4096]{2,1,0:T(8,128)(2,1)} %param.7) | copy-start | bytes 1572868
  0.6 18.3 %collective-permute-start = (bf16[64,4096]{1,0:T(8,128)(2,1)}, bf16[64,4096]{1,0:T(8,128)(2,1)S(1)}, u32[]{:S(2)}, u32[]{:S(2)}) collective-permute-start(bf16[64,4096]{1,0:T(8,128)(2,1)} %bitcast.31), channel_id=1, source_target_pairs={{0,16},{8,24},{16,32},{24,40},{32,48},{40,56},{48,64},{56,72},{64,... | collective-permute-start | bytes 1572872 | tf_op jit(solution)/shard_map/ppermute | solution.py:51
  3.2 15.8 %collective-permute-start.1 = (bf16[64,4096]{1,0:T(8,128)(2,1)}, bf16[64,4096]{1,0:T(8,128)(2,1)}, u32[]{:S(2)}, u32[]{:S(2)}) collective-permute-start(bf16[64,4096]{1,0:T(8,128)(2,1)} %bitcast.32), channel_id=1, source_target_pairs={{0,112},{8,120},{16,0},{24,8},{32,16},{40,24},{48,32},{56,40},{64,... | collective-permute-start | bytes 1572872 | tf_op jit(solution)/shard_map/ppermute | solution.py:51
  7.2 14.2 %collective-permute-start.2 = (bf16[64,4096]{1,0:T(8,128)(2,1)}, bf16[64,4096]{1,0:T(8,128)(2,1)S(1)}, u32[]{:S(2)}, u32[]{:S(2)}) collective-permute-start(bf16[64,4096]{1,0:T(8,128)(2,1)} %bitcast.33), channel_id=1, source_target_pairs={{0,128},{8,136},{16,144},{24,152},{32,160},{40,168},{48,176},{56,1... | collective-permute-start | bytes 1572872 | tf_op jit(solution)/shard_map/ppermute | solution.py:51
  13.3 2.5 %collective-permute-start.3 = (f32[32,2176]{1,0:T(8,128)S(1)}, f32[32,2176]{1,0:T(8,128)S(1)}, u32[]{:S(2)}, u32[]{:S(2)}) collective-permute-start(f32[32,2176]{1,0:T(8,128)S(1)} %get-tuple-element.30), channel_id=1, source_target_pairs={{0,8},{8,0},{16,24},{24,16},{32,40},{40,32},{48,56},{56,48},{64,72... | collective-permute-start | bytes 835592 | tf_op jit(solution)/shard_map/ppermute | solution.py:51
  14.6 9.2 %collective-permute-start.7 = (bf16[64,4096]{1,0:T(8,128)(2,1)S(1)}, bf16[64,4096]{1,0:T(8,128)(2,1)S(1)}, u32[]{:S(2)}, u32[]{:S(2)}) collective-permute-start(bf16[64,4096]{1,0:T(8,128)(2,1)S(1)} %bitcast.36), channel_id=1, source_target_pairs={{0,8},{8,0},{16,24},{24,16},{32,40},{40,32},{48,56},{56,48},{64,72... | collective-permute-start | bytes 1572872 | tf_op jit(solution)/shard_map/ppermute | solution.py:51
  19.0 18.8 %copy-start.7 = (bf16[64,4096]{1,0:T(8,128)(2,1)}, bf16[64,4096]{1,0:T(8,128)(2,1)S(1)}, u32[]{:S(2)}) copy-start(bf16[64,4096]{1,0:T(8,128)(2,1)S(1)} %collective-permute-done.refs_2_) | copy-start | bytes 1572868
  21.4 5.0 %collective-permute-start.10 = (bf16[64,4096]{1,0:T(8,128)(2,1)S(1)}, bf16[64,4096]{1,0:T(8,128)(2,1)}, u32[]{:S(2)}, u32[]{:S(2)}) collective-permute-start(bf16[64,4096]{1,0:T(8,128)(2,1)S(1)} %collective-permute-done.2.refs_6_), channel_id=1, source_target_pairs={{0,8},{8,0},{16,24},{24,16},{32,40},{40,32},{48,56},{56,48},{64,72... | collective-permute-start | bytes 1572872 | tf_op jit(solution)/shard_map/ppermute | solution.py:51
  23.3 11.6 %collective-permute-start.8 = (bf16[64,4096]{1,0:T(8,128)(2,1)S(1)}, bf16[64,4096]{1,0:T(8,128)(2,1)}, u32[]{:S(2)}, u32[]{:S(2)}) collective-permute-start(bf16[64,4096]{1,0:T(8,128)(2,1)S(1)} %collective-permute-done.refs_2_), channel_id=1, source_target_pairs={{0,8},{8,0},{16,24},{24,16},{32,40},{40,32},{48,56},{56,48},{64,72... | collective-permute-start | bytes 1572872 | tf_op jit(solution)/shard_map/ppermute | solution.py:51
  23.3 14.5 %collective-permute-start.9 = (bf16[64,4096]{1,0:T(8,128)(2,1)}, bf16[64,4096]{1,0:T(8,128)(2,1)}, u32[]{:S(2)}, u32[]{:S(2)}) collective-permute-start(bf16[64,4096]{1,0:T(8,128)(2,1)} %collective-permute-done.1.refs_4_), channel_id=1, source_target_pairs={{0,8},{8,0},{16,24},{24,16},{32,40},{40,32},{48,56},{56,48},{64,72... | collective-permute-start | bytes 1572872 | tf_op jit(solution)/shard_map/ppermute | solution.py:51
  23.8 20.2 %collective-permute-start.4 = (bf16[64,4096]{1,0:T(8,128)(2,1)S(1)}, bf16[64,4096]{1,0:T(8,128)(2,1)S(1)}, u32[]{:S(2)}, u32[]{:S(2)}) collective-permute-start(bf16[64,4096]{1,0:T(8,128)(2,1)S(1)} %collective-permute-done.refs_2_), channel_id=1, source_target_pairs={{0,16},{8,24},{16,32},{24,40},{32,48},{40,56},{48,64},{56,72},{64,... | collective-permute-start | bytes 1572872 | tf_op jit(solution)/shard_map/ppermute | solution.py:51
  23.8 11.0 %copy-start.10 = (bf16[64,4096]{1,0:T(8,128)(2,1)}, bf16[64,4096]{1,0:T(8,128)(2,1)S(1)}, u32[]{:S(2)}) copy-start(bf16[64,4096]{1,0:T(8,128)(2,1)S(1)} %collective-permute-done.7.refs_1_) | copy-start | bytes 1572868
  23.8 20.3 %collective-permute-start.5 = (bf16[64,4096]{1,0:T(8,128)(2,1)}, bf16[64,4096]{1,0:T(8,128)(2,1)S(1)}, u32[]{:S(2)}, u32[]{:S(2)}) collective-permute-start(bf16[64,4096]{1,0:T(8,128)(2,1)} %collective-permute-done.1.refs_4_), channel_id=1, source_target_pairs={{0,112},{8,120},{16,0},{24,8},{32,16},{40,24},{48,32},{56,40},{64,... | collective-permute-start | bytes 1572872 | tf_op jit(solution)/shard_map/ppermute | solution.py:51
  26.5 17.6 %collective-permute-start.6 = (bf16[64,4096]{1,0:T(8,128)(2,1)}, bf16[64,4096]{1,0:T(8,128)(2,1)S(1)}, u32[]{:S(2)}, u32[]{:S(2)}) collective-permute-start(bf16[64,4096]{1,0:T(8,128)(2,1)} %collective-permute-done.1.refs_4_), channel_id=1, source_target_pairs={{0,128},{8,136},{16,144},{24,152},{32,160},{40,168},{48,176},{56,1... | collective-permute-start | bytes 1572872 | tf_op jit(solution)/shard_map/ppermute | solution.py:51
  29.4 20.9 %all-to-all-start = ((f32[16,64,128]{2,1,0:T(8,128)}), f32[16,64,128]{2,1,0:T(8,128)S(1)}, u32[]{:S(2)}, u32[]{:S(2)}) async-start(f32[16,64,128]{2,1,0:T(8,128)} %pack.1), calls=%async_computation | async-start | bytes 1048576 | tf_op jit(solution)/shard_map/all_to_all | solution.py:344
  34.9 21.8 %copy-start = (s32[1,2048]{1,0:T(1,128)S(1)}, s32[1,2048]{1,0:T(1,128)}, u32[]{:S(2)}) copy-start(s32[1,2048]{1,0:T(1,128)} %ids_ref.1) | copy-start | bytes 24580
  34.9 23.4 %collective-permute-start.13 = (bf16[64,4096]{1,0:T(8,128)(2,1)S(1)}, bf16[64,4096]{1,0:T(8,128)(2,1)S(1)}, u32[]{:S(2)}, u32[]{:S(2)}) collective-permute-start(bf16[64,4096]{1,0:T(8,128)(2,1)S(1)} %collective-permute-done.refs_2_), channel_id=1, source_target_pairs={{0,128},{8,136},{16,144},{24,152},{32,160},{40,168},{48,176},{56,1... | collective-permute-start | bytes 1572872 | tf_op jit(solution)/shard_map/ppermute | solution.py:51
  44.1 31.4 %copy-start.3 = (bf16[64,4096]{1,0:T(8,128)(2,1)}, bf16[64,4096]{1,0:T(8,128)(2,1)S(1)}, u32[]{:S(2)}) copy-start(bf16[64,4096]{1,0:T(8,128)(2,1)S(1)} %collective-permute-done.4.refs_0_) | copy-start | bytes 1572868
  44.1 31.4 %copy-start.2 = (bf16[64,4096]{1,0:T(8,128)(2,1)}, bf16[64,4096]{1,0:T(8,128)(2,1)S(1)}, u32[]{:S(2)}) copy-start(bf16[64,4096]{1,0:T(8,128)(2,1)S(1)} %collective-permute-done.5.refs_2_) | copy-start | bytes 1572868
  44.1 31.4 %copy-start.4 = (bf16[64,4096]{1,0:T(8,128)(2,1)}, bf16[64,4096]{1,0:T(8,128)(2,1)S(1)}, u32[]{:S(2)}) copy-start(bf16[64,4096]{1,0:T(8,128)(2,1)S(1)} %collective-permute-done.6.refs_4_) | copy-start | bytes 1572868
  44.1 16.5 %collective-permute-start.11 = (bf16[64,4096]{1,0:T(8,128)(2,1)S(1)}, bf16[64,4096]{1,0:T(8,128)(2,1)}, u32[]{:S(2)}, u32[]{:S(2)}) collective-permute-start(bf16[64,4096]{1,0:T(8,128)(2,1)S(1)} %collective-permute-done.4.refs_0_), channel_id=1, source_target_pairs={{0,16},{8,24},{16,32},{24,40},{32,48},{40,56},{48,64},{56,72},{64,... | collective-permute-start | bytes 1572872 | tf_op jit(solution)/shard_map/ppermute | solution.py:51
  45.4 15.3 %collective-permute-start.12 = (bf16[64,4096]{1,0:T(8,128)(2,1)S(1)}, bf16[64,4096]{1,0:T(8,128)(2,1)}, u32[]{:S(2)}, u32[]{:S(2)}) collective-permute-start(bf16[64,4096]{1,0:T(8,128)(2,1)S(1)} %collective-permute-done.5.refs_2_), channel_id=1, source_target_pairs={{0,112},{8,120},{16,0},{24,8},{32,16},{40,24},{48,32},{56,40},{64,... | collective-permute-start | bytes 1572872 | tf_op jit(solution)/shard_map/ppermute | solution.py:51
  50.8 5.5 %collective-permute-start.14 = (f32[32,128]{1,0:T(8,128)S(1)}, f32[32,128]{1,0:T(8,128)S(1)}, u32[]{:S(2)}, u32[]{:S(2)}) collective-permute-start(f32[32,128]{1,0:T(8,128)S(1)} %left.1.left_ref), channel_id=1, source_target_pairs={{0,8},{8,0},{16,24},{24,16},{32,40},{40,32},{48,56},{56,48},{64,72... | collective-permute-start | bytes 49160 | tf_op jit(solution)/shard_map/ppermute | solution.py:51
  55.5 9.3 %collective-permute-start.18 = (bf16[64,4096]{1,0:T(8,128)(2,1)S(1)}, bf16[64,4096]{1,0:T(8,128)(2,1)S(1)}, u32[]{:S(2)}, u32[]{:S(2)}) collective-permute-start(bf16[64,4096]{1,0:T(8,128)(2,1)S(1)} %collective-permute-done.4.refs_0_), channel_id=1, source_target_pairs={{0,8},{8,0},{16,24},{24,16},{32,40},{40,32},{48,56},{56,48},{64,72... | collective-permute-start | bytes 1572872 | tf_op jit(solution)/shard_map/ppermute | solution.py:51
  56.3 8.5 %collective-permute-start.19 = (bf16[64,4096]{1,0:T(8,128)(2,1)S(1)}, bf16[64,4096]{1,0:T(8,128)(2,1)S(1)}, u32[]{:S(2)}, u32[]{:S(2)}) collective-permute-start(bf16[64,4096]{1,0:T(8,128)(2,1)S(1)} %collective-permute-done.5.refs_2_), channel_id=1, source_target_pairs={{0,8},{8,0},{16,24},{24,16},{32,40},{40,32},{48,56},{56,48},{64,72... | collective-permute-start | bytes 1572872 | tf_op jit(solution)/shard_map/ppermute | solution.py:51
  58.3 23.5 %copy-start.6 = (bf16[64,4096]{1,0:T(8,128)(2,1)}, bf16[64,4096]{1,0:T(8,128)(2,1)S(1)}, u32[]{:S(2)}) copy-start(bf16[64,4096]{1,0:T(8,128)(2,1)S(1)} %collective-permute-done.13.refs_2_) | copy-start | bytes 1572868
  58.3 9.5 %collective-permute-start.20 = (bf16[64,4096]{1,0:T(8,128)(2,1)S(1)}, bf16[64,4096]{1,0:T(8,128)(2,1)S(1)}, u32[]{:S(2)}, u32[]{:S(2)}) collective-permute-start(bf16[64,4096]{1,0:T(8,128)(2,1)S(1)} %collective-permute-done.6.refs_4_), channel_id=1, source_target_pairs={{0,8},{8,0},{16,24},{24,16},{32,40},{40,32},{48,56},{56,48},{64,72... | collective-permute-start | bytes 1572872 | tf_op jit(solution)/shard_map/ppermute | solution.py:51
  60.6 7.8 %collective-permute-start.21 = (bf16[64,4096]{1,0:T(8,128)(2,1)}, bf16[64,4096]{1,0:T(8,128)(2,1)S(1)}, u32[]{:S(2)}, u32[]{:S(2)}) collective-permute-start(bf16[64,4096]{1,0:T(8,128)(2,1)} %collective-permute-done.11.refs_6_), channel_id=1, source_target_pairs={{0,8},{8,0},{16,24},{24,16},{32,40},{40,32},{48,56},{56,48},{64,72... | collective-permute-start | bytes 1572872 | tf_op jit(solution)/shard_map/ppermute | solution.py:51
  61.9 19.8 %collective-permute-start.17 = (bf16[64,4096]{1,0:T(8,128)(2,1)S(1)}, bf16[64,4096]{1,0:T(8,128)(2,1)S(1)}, u32[]{:S(2)}, u32[]{:S(2)}) collective-permute-start(bf16[64,4096]{1,0:T(8,128)(2,1)S(1)} %collective-permute-done.5.refs_2_), channel_id=1, source_target_pairs={{0,128},{8,136},{16,144},{24,152},{32,160},{40,168},{48,176},{56,1... | collective-permute-start | bytes 1572872 | tf_op jit(solution)/shard_map/ppermute | solution.py:51
  64.8 19.5 %collective-permute-start.15 = (bf16[64,4096]{1,0:T(8,128)(2,1)S(1)}, bf16[64,4096]{1,0:T(8,128)(2,1)S(1)}, u32[]{:S(2)}, u32[]{:S(2)}) collective-permute-start(bf16[64,4096]{1,0:T(8,128)(2,1)S(1)} %collective-permute-done.13.refs_2_), channel_id=1, source_target_pairs={{0,16},{8,24},{16,32},{24,40},{32,48},{40,56},{48,64},{56,72},{64,... | collective-permute-start | bytes 1572872 | tf_op jit(solution)/shard_map/ppermute | solution.py:51
  64.9 19.4 %collective-permute-start.16 = (bf16[64,4096]{1,0:T(8,128)(2,1)}, bf16[64,4096]{1,0:T(8,128)(2,1)}, u32[]{:S(2)}, u32[]{:S(2)}) collective-permute-start(bf16[64,4096]{1,0:T(8,128)(2,1)} %collective-permute-done.12.refs_0_), channel_id=1, source_target_pairs={{0,112},{8,120},{16,0},{24,8},{32,16},{40,24},{48,32},{56,40},{64,... | collective-permute-start | bytes 1572872 | tf_op jit(solution)/shard_map/ppermute | solution.py:51
  67.8 18.8 %collective-permute-start.26 = (bf16[64,4096]{1,0:T(8,128)(2,1)}, bf16[64,4096]{1,0:T(8,128)(2,1)}, u32[]{:S(2)}, u32[]{:S(2)}) collective-permute-start(bf16[64,4096]{1,0:T(8,128)(2,1)} %collective-permute-done.12.refs_0_), channel_id=1, source_target_pairs={{0,8},{8,0},{16,24},{24,16},{32,40},{40,32},{48,56},{56,48},{64,72... | collective-permute-start | bytes 1572872 | tf_op jit(solution)/shard_map/ppermute | solution.py:51
  69.4 19.1 %collective-permute-start.27 = (bf16[64,4096]{1,0:T(8,128)(2,1)S(1)}, bf16[64,4096]{1,0:T(8,128)(2,1)}, u32[]{:S(2)}, u32[]{:S(2)}) collective-permute-start(bf16[64,4096]{1,0:T(8,128)(2,1)S(1)} %collective-permute-done.13.refs_2_), channel_id=1, source_target_pairs={{0,8},{8,0},{16,24},{24,16},{32,40},{40,32},{48,56},{56,48},{64,72... | collective-permute-start | bytes 1572872 | tf_op jit(solution)/shard_map/ppermute | solution.py:51
  70.0 14.3 %all-to-all-start.1 = ((f32[16,8,128]{2,1,0:T(8,128)}), f32[16,8,128]{2,1,0:T(8,128)S(1)}, u32[]{:S(2)}, u32[]{:S(2)}) async-start(f32[16,8,128]{2,1,0:T(8,128)} %feats.1), calls=%async_computation.1 | async-start | bytes 131072 | tf_op jit(solution)/shard_map/all_to_all | solution.py:367
  81.8 21.5 %copy-start.5 = (bf16[64,4096]{1,0:T(8,128)(2,1)}, bf16[64,4096]{1,0:T(8,128)(2,1)S(1)}, u32[]{:S(2)}) copy-start(bf16[64,4096]{1,0:T(8,128)(2,1)S(1)} %collective-permute-done.17.refs_0_) | copy-start | bytes 1572868
  84.3 12.7 %copy-start.8 = (bf16[64,4096]{1,0:T(8,128)(2,1)}, bf16[64,4096]{1,0:T(8,128)(2,1)S(1)}, u32[]{:S(2)}) copy-start(bf16[64,4096]{1,0:T(8,128)(2,1)S(1)} %collective-permute-done.15.refs_4_) | copy-start | bytes 1572868
  84.3 11.1 %collective-permute-start.28 = (bf16[64,4096]{1,0:T(8,128)(2,1)S(1)}, bf16[64,4096]{1,0:T(8,128)(2,1)S(1)}, u32[]{:S(2)}, u32[]{:S(2)}) collective-permute-start(bf16[64,4096]{1,0:T(8,128)(2,1)S(1)} %collective-permute-done.15.refs_4_), channel_id=1, source_target_pairs={{0,8},{8,0},{16,24},{24,16},{32,40},{40,32},{48,56},{56,48},{64,72... | collective-permute-start | bytes 1572872 | tf_op jit(solution)/shard_map/ppermute | solution.py:51
  85.7 11.3 %collective-permute-start.29 = (bf16[64,4096]{1,0:T(8,128)(2,1)}, bf16[64,4096]{1,0:T(8,128)(2,1)}, u32[]{:S(2)}, u32[]{:S(2)}) collective-permute-start(bf16[64,4096]{1,0:T(8,128)(2,1)} %collective-permute-done.16.refs_6_), channel_id=1, source_target_pairs={{0,8},{8,0},{16,24},{24,16},{32,40},{40,32},{48,56},{56,48},{64,72... | collective-permute-start | bytes 1572872 | tf_op jit(solution)/shard_map/ppermute | solution.py:51
  85.8 21.7 %collective-permute-start.23 = (bf16[64,4096]{1,0:T(8,128)(2,1)S(1)}, bf16[64,4096]{1,0:T(8,128)(2,1)}, u32[]{:S(2)}, u32[]{:S(2)}) collective-permute-start(bf16[64,4096]{1,0:T(8,128)(2,1)S(1)} %collective-permute-done.15.refs_4_), channel_id=1, source_target_pairs={{0,16},{8,24},{16,32},{24,40},{32,48},{40,56},{48,64},{56,72},{64,... | collective-permute-start | bytes 1572872 | tf_op jit(solution)/shard_map/ppermute | solution.py:51
  86.7 20.8 %collective-permute-start.24 = (bf16[64,4096]{1,0:T(8,128)(2,1)S(1)}, bf16[64,4096]{1,0:T(8,128)(2,1)}, u32[]{:S(2)}, u32[]{:S(2)}) collective-permute-start(bf16[64,4096]{1,0:T(8,128)(2,1)S(1)} %collective-permute-done.17.refs_0_), channel_id=1, source_target_pairs={{0,112},{8,120},{16,0},{24,8},{32,16},{40,24},{48,32},{56,40},{64,... | collective-permute-start | bytes 1572872 | tf_op jit(solution)/shard_map/ppermute | solution.py:51
  88.5 19.0 %collective-permute-start.25 = (bf16[64,4096]{1,0:T(8,128)(2,1)}, bf16[64,4096]{1,0:T(8,128)(2,1)S(1)}, u32[]{:S(2)}, u32[]{:S(2)}) collective-permute-start(bf16[64,4096]{1,0:T(8,128)(2,1)} %collective-permute-done.16.refs_6_), channel_id=1, source_target_pairs={{0,128},{8,136},{16,144},{24,152},{32,160},{40,168},{48,176},{56,1... | collective-permute-start | bytes 1572872 | tf_op jit(solution)/shard_map/ppermute | solution.py:51
  91.1 16.4 %all-to-all-start.2 = ((f32[8,128,128]{2,1,0:T(8,128)}), f32[8,128,128]{2,1,0:T(8,128)S(1)}, u32[]{:S(2)}, u32[]{:S(2)}) async-start(f32[8,128,128]{2,1,0:T(8,128)} %broadcast_in_dim.11), calls=%async_computation.2 | async-start | bytes 1048576 | tf_op jit(solution)/shard_map/all_to_all | solution.py:376
  95.4 23.8 %collective-permute-start.22 = (bf16[64,4096]{1,0:T(8,128)(2,1)S(1)}, bf16[64,4096]{1,0:T(8,128)(2,1)}, u32[]{:S(2)}, u32[]{:S(2)}) collective-permute-start(bf16[64,4096]{1,0:T(8,128)(2,1)S(1)} %collective-permute-done.17.refs_0_), channel_id=1, source_target_pairs={{0,8},{8,0},{16,24},{24,16},{32,40},{40,32},{48,56},{56,48},{64,72... | collective-permute-start | bytes 1572872 | tf_op jit(solution)/shard_map/ppermute | solution.py:51
  107.5 11.7 %copy-start.11 = (bf16[64,4096]{1,0:T(8,128)(2,1)}, bf16[64,4096]{1,0:T(8,128)(2,1)S(1)}, u32[]{:S(2)}) copy-start(bf16[64,4096]{1,0:T(8,128)(2,1)S(1)} %collective-permute-done.25.refs_6_) | copy-start | bytes 1572868
  107.5 3.5 %collective-permute-start.33 = (f32[8,128,128]{2,1,0:T(8,128)S(1)}, f32[8,128,128]{2,1,0:T(8,128)S(1)}, u32[]{:S(2)}, u32[]{:S(2)}) collective-permute-start(f32[8,128,128]{2,1,0:T(8,128)S(1)} %all-to-all-done.2.mine_ref), channel_id=1, source_target_pairs={{0,8},{8,0},{16,24},{24,16},{32,40},{40,32},{48,56},{56,48},{64,72... | collective-permute-start | bytes 1572872 | tf_op jit(solution)/shard_map/ppermute | solution.py:51
  109.5 9.7 %collective-permute-start.30 = (bf16[64,4096]{1,0:T(8,128)(2,1)}, bf16[64,4096]{1,0:T(8,128)(2,1)S(1)}, u32[]{:S(2)}, u32[]{:S(2)}) collective-permute-start(bf16[64,4096]{1,0:T(8,128)(2,1)} %collective-permute-done.23.refs_2_), channel_id=1, source_target_pairs={{0,8},{8,0},{16,24},{24,16},{32,40},{40,32},{48,56},{56,48},{64,72... | collective-permute-start | bytes 1572872 | tf_op jit(solution)/shard_map/ppermute | solution.py:51
  109.8 9.3 %collective-permute-start.31 = (bf16[64,4096]{1,0:T(8,128)(2,1)}, bf16[64,4096]{1,0:T(8,128)(2,1)}, u32[]{:S(2)}, u32[]{:S(2)}) collective-permute-start(bf16[64,4096]{1,0:T(8,128)(2,1)} %collective-permute-done.24.refs_4_), channel_id=1, source_target_pairs={{0,8},{8,0},{16,24},{24,16},{32,40},{40,32},{48,56},{56,48},{64,72... | collective-permute-start | bytes 1572872 | tf_op jit(solution)/shard_map/ppermute | solution.py:51
  110.0 9.2 %collective-permute-start.32 = (bf16[64,4096]{1,0:T(8,128)(2,1)S(1)}, bf16[64,4096]{1,0:T(8,128)(2,1)}, u32[]{:S(2)}, u32[]{:S(2)}) collective-permute-start(bf16[64,4096]{1,0:T(8,128)(2,1)S(1)} %collective-permute-done.25.refs_6_), channel_id=1, source_target_pairs={{0,8},{8,0},{16,24},{24,16},{32,40},{40,32},{48,56},{56,48},{64,72... | collective-permute-start | bytes 1572872 | tf_op jit(solution)/shard_map/ppermute | solution.py:51
  (7 other events, 19.1 us)

commit v2 on v1

--- a/solution.py
+++ b/solution.py
@@ -242,7 +242,23 @@
     out_ref[...] = jnp.broadcast_to(wide[None], out_ref.shape)
 
 
-def finish_kernel(examples, info_ref, mine_ref, other_ref, gram_ref, scores_ref, full):
+def finish_kernel(examples, count, info_ref, place_ref, mine_ref, other_ref, weight_hbm, *refs):
+    block_refs = refs[: 2 * count]
+    out_ref, gram_ref, scores_ref, full, weight, tokens, total, rounded, load_sems, out_sems = refs[
+        2 * count + 1 :
+    ]
+    loads = [pltpu.make_async_copy(weight_hbm, weight, load_sems.at[2 * count])]
+    for b in range(count):
+        for side in range(2):
+            half = info_ref[0] if side == 0 else 1 - info_ref[0]
+            start = pl.multiple_of(b * LANES + half * 64, 64)
+            loads.append(
+                pltpu.make_async_copy(
+                    block_refs[2 * b + side], tokens.at[pl.ds(start, 64)], load_sems.at[2 * b + side]
+                )
+            )
+    for load in loads:
+        load.start()
     core, device, group = info_ref[0], info_ref[1], info_ref[2]
     for chip in range(CHIPS):
         rows = slice(chip * EX_GRP, (chip + 1) * EX_GRP)
@@ -264,11 +280,11 @@
 
     cols = columns(device % CHIPS, device // CHIPS)
     per_group = CHIPS // 4
-    rows = jnp.concatenate(
+    gram_rows = jnp.concatenate(
         [columns(per_group * (group % 4) + q, group // 4) for q in range(per_group)], axis=1
     )
     gram_ref[...] = (
-        lax.dot_general(rows, cols, TN, precision=EXACT, preferred_element_type=jnp.float32)
+        lax.dot_general(gram_rows, cols, TN, precision=EXACT, preferred_element_type=jnp.float32)
         / examples
     )
     kernel = lax.dot_general(
@@ -279,14 +295,43 @@
     diagonal = sub == lane
     ridge = jnp.sum(jnp.where(diagonal, kernel, 0.0)) / examples
     matrix = jnp.where(diagonal, kernel + ridge, kernel)
-    for k in range(examples):
-        column = matrix[:, k : k + 1]
-        pivot = matrix[k : k + 1, k : k + 1]
-        row = jnp.where(lane[:1] == k, 1.0, matrix[k : k + 1, :]) / pivot
-        cleared = jnp.where(lane == k, 0.0, matrix) - column * row
-        matrix = jnp.where(sub == k, row, cleared)
+    for load in loads:
+        load.wait()
+    pieces = 8
+    depth = weight.shape[1] // pieces
+    for piece in range(pieces):
+        part = slice(piece * depth, (piece + 1) * depth)
+        product = lax.dot_general(
+            weight[:, part], tokens[:, part], NT, preferred_element_type=jnp.float32
+        )
+        if piece == 0:
+            total[...] = product
+        elif piece < pieces - 1:
+            total[...] += product
+        else:
+            rounded[...] = (total[...] + product).astype(jnp.bfloat16)
+        for k in range(piece * examples // pieces, (piece + 1) * examples // pieces):
+            column = matrix[:, k : k + 1]
+            pivot = matrix[k : k + 1, k : k + 1]
+            row = jnp.where(lane[:1] == k, 1.0, matrix[k : k + 1, :]) / pivot
+            cleared = jnp.where(lane == k, 0.0, matrix) - column * row
+            matrix = jnp.where(sub == k, row, cleared)
+    stores = []
+    for b in range(count):
+        place = pl.multiple_of(place_ref[b] * LANES, LANES)
+        stores.append(
+            pltpu.make_async_copy(
+                rounded.at[:, pl.ds(b * LANES, LANES)],
+                out_ref.at[:, pl.ds(place, LANES)],
+                out_sems.at[b],
+            )
+        )
+    for store in stores:
+        store.start()
     inverse = jnp.sum(jnp.where(diagonal, matrix, 0.0), axis=0, keepdims=True)
     scores_ref[...] = 1.0 - ridge * inverse
+    for store in stores:
+        store.wait()
 
 
 def body(hidden_act, grad_output, down_weight, proj_in, proj_out, example_ids):
@@ -389,22 +434,39 @@
     far_below3, far_above3, far_above4, out, feats = tie(
         (far_below3, far_above3, far_above4, out, feats)
     )
-    out = columns(
-        out,
+    last = [
+        (far_above2, chip(away, 2)),
+        (far_below3, chip(away, -3)),
+        (far_above3, chip(away, 3)),
+        (far_above4, chip(away, 4)),
+    ]
+    pairs = [rows for block, _ in last for rows in (block, permute(block, SWAP))]
+    args = [info, jnp.stack([place for _, place in last]).astype(jnp.int32), feats]
+    args += [permute(feats, SWAP), *map(in_hbm, [down_weight, *pairs]), out]
+    width, depth = down_weight.shape
+    wide = len(last) * LANES
+    out, gram, scores = call(
+        functools.partial(finish_kernel, examples, len(last)),
+        "finish",
+        18,
+        (
+            jax.ShapeDtypeStruct(out.shape, out.dtype),
+            f32(PROJ * PROJ // group_count, LANES),
+            f32(1, examples),
+        ),
+        args,
         [
-            (far_above2, away, 2),
-            (far_below3, away, -3),
-            (far_above3, away, 3),
-            (far_above4, away, 4),
+            pltpu.VMEM((examples, PROJ * PROJ), jnp.float32),
+            pltpu.VMEM((width, depth), jnp.bfloat16),
+            pltpu.VMEM((wide, depth), jnp.bfloat16),
+            pltpu.VMEM((width, wide), jnp.float32),
+            pltpu.VMEM((width, wide), jnp.bfloat16),
+            pltpu.SemaphoreType.DMA((2 * len(last) + 1,)),
+            pltpu.SemaphoreType.DMA((len(last),)),
         ],
-    )
-    gram, scores = call(
-        functools.partial(finish_kernel, examples),
-        "finish",
-        12,
-        (f32(PROJ * PROJ // group_count, LANES), f32(1, examples)),
-        [info, feats, permute(feats, SWAP)],
-        [pltpu.VMEM((examples, PROJ * PROJ), jnp.float32)],
+        [SMEM, SMEM, VMEM, VMEM] + [ANY] * (len(pairs) + 2),
+        (ANY, VMEM, VMEM),
+        {len(args) - 1: 0},
     )
     return (jnp.transpose(out)[None], gram, scores[0])
 

time: 127 us -> 125 us (0.984)
  Pallas kernels: 40 us -> 36.4 us
  waiting for transfers between devices: 17.9 us -> 20.2 us
    pallas_call x9 -> x8, Pallas kernels: 40 us -> 36.4 us  [call(): pl.pallas_call(kernel, name=name, out_shape=out_shape, in_specs=in_specs...]
    ppermute x34, waiting for transfers between devices: 7.71 us -> 9.91 us  [permute(): return lax.ppermute(value, 'fsdp', pairs)]
  transfers between devices with their start and end apart: 37 -> 37, of which waited for: 9 -> 12; matrix products, arithmetic and copies ran while one was open for 1% -> 1% of each run, Pallas kernels for 27% -> 20%
where the time goes in v2:
time: 125 us
  starting transfers between devices  63.9 us (51%)
  Pallas kernels  36.4 us (29%)
  waiting for transfers between devices  20.2 us (16%)
  local copies, waits for them, and re-layouts  2.73 us (2%)
    ppermute x34, starting transfers between devices, permute(): return lax.ppermute(value, 'fsdp', pairs)  49.3 us
    pallas_call x8, Pallas kernels, call(): pl.pallas_call(kernel, name=name, out_shape=out_shape, in_specs=in_specs...  36.4 us
    ppermute x34, waiting for transfers between devices, permute(): return lax.ppermute(value, 'fsdp', pairs)  9.91 us
    all_to_all x1, starting transfers between devices, body(): lax.all_to_all(packed, 'fsdp', 0, 0, axis_index_groups=SAME_CORE, tiled=T...  5.3 us
    all_to_all x1, starting transfers between devices, body(): lax.all_to_all(feats, 'fsdp', 0, 0, axis_index_groups=SAME_CORE, tiled=True)  5.15 us
    all_to_all x1, waiting for transfers between devices, body(): lax.all_to_all(jnp.broadcast_to(feats.reshape(1, CHIPS * EX_GRP, LANES),...  4.32 us
    all_to_all x1, starting transfers between devices, body(): lax.all_to_all(jnp.broadcast_to(feats.reshape(1, CHIPS * EX_GRP, LANES),...  4.14 us
    all_to_all x1, waiting for transfers between devices, body(): lax.all_to_all(packed, 'fsdp', 0, 0, axis_index_groups=SAME_CORE, tiled=T...  3.44 us
  transfers between devices with their start and end apart: 37, of which 12 were waited for; matrix products, arithmetic and copies ran while one was open for 1% of the time, Pallas kernels for 20%

profile of v2, /device:TPU:1, one launch (start us, length us, event | category | flops | bytes accessed | tf_op | source)
XLA Modules:
  0.0 124.6 jit_solution(3996111703311400754)
XLA Ops:
  0.6 2.5 %collective-permute-start = (bf16[64,4096]{1,0:T(8,128)(2,1)}, bf16[64,4096]{1,0:T(8,128)(2,1)}, u32[]{:S(2)}, u32[]{:S(2)}) collective-permute-start(bf16[64,4096]{1,0:T(8,128)(2,1)} %bitcast.31), channel_id=1, source_target_pairs={{0,16},{8,24},{16,32},{24,40},{32,48},{40,56},{48,64},{56,72},{64,... | collective-permute-start | bytes 1572872 | tf_op jit(solution)/shard_map/ppermute | solution.py:51
  3.2 4.0 %collective-permute-start.1 = (bf16[64,4096]{1,0:T(8,128)(2,1)}, bf16[64,4096]{1,0:T(8,128)(2,1)}, u32[]{:S(2)}, u32[]{:S(2)}) collective-permute-start(bf16[64,4096]{1,0:T(8,128)(2,1)} %bitcast.32), channel_id=1, source_target_pairs={{0,112},{8,120},{16,0},{24,8},{32,16},{40,24},{48,32},{56,40},{64,... | collective-permute-start | bytes 1572872 | tf_op jit(solution)/shard_map/ppermute | solution.py:51
  7.2 2.9 %collective-permute-start.2 = (bf16[64,4096]{1,0:T(8,128)(2,1)}, bf16[64,4096]{1,0:T(8,128)(2,1)S(1)}, u32[]{:S(2)}, u32[]{:S(2)}) collective-permute-start(bf16[64,4096]{1,0:T(8,128)(2,1)} %bitcast.33), channel_id=1, source_target_pairs={{0,128},{8,136},{16,144},{24,152},{32,160},{40,168},{48,176},{56,1... | collective-permute-start | bytes 1572872 | tf_op jit(solution)/shard_map/ppermute | solution.py:51
  10.2 3.1 %project.1 = (f32[32,2176]{1,0:T(8,128)S(1)}, f32[32,2176]{1,0:T(8,128)S(1)}) custom-call(s32[3]{0:T(128)S(1)} %pad_add_fusion.info_ref, bf16[448,2048]{1,0:T(8,128)(2,1)} %bitcast.37, bf16[64,448]{1,0:T(8,128)(2,1)} %bitcast.40, bf16[64,4096]{1,0:T(8,128)(2,1)} %bitcast.34, bf16[64,4096]{1,0:T(8,128)(2,1)} %bitcast.38), custom_call_target="tpu_custom_call" | custom-call | tf_op jit(solution)/shard_map/project/pallas_call | solution.py:57
  13.3 1.3 %collective-permute-start.3 = (f32[32,2176]{1,0:T(8,128)S(1)}, f32[32,2176]{1,0:T(8,128)S(1)}, u32[]{:S(2)}, u32[]{:S(2)}) collective-permute-start(f32[32,2176]{1,0:T(8,128)S(1)} %get-tuple-element.31), channel_id=1, source_target_pairs={{0,8},{8,0},{16,24},{24,16},{32,40},{40,32},{48,56},{56,48},{64,72... | collective-permute-start | bytes 835592 | tf_op jit(solution)/shard_map/ppermute | solution.py:51
  14.7 1.1 collective-permute-done.3.taken_ref
  15.8 1.5 %pack.1 = f32[16,64,128]{2,1,0:T(8,128)} custom-call(s32[3]{0:T(128)S(1)} %pad_add_fusion.info_ref, f32[32,2176]{1,0:T(8,128)S(1)} %get-tuple-element.30.kept_ref, f32[32,2176]{1,0:T(8,128)S(1)} %collective-permute-done.3.taken_ref), custom_call_target="tpu_custom_call" | custom-call | tf_op jit(solution)/shard_map/pack/pallas_call | solution.py:57
  17.3 1.8 %collective-permute-done.refs_2_ = bf16[64,4096]{1,0:T(8,128)(2,1)} collective-permute-done((bf16[64,4096]{1,0:T(8,128)(2,1)}, bf16[64,4096]{1,0:T(8,128)(2,1)}, u32[]{:S(2)}, u32[]{:S(2)}) %collective-permute-start) | collective-permute-done | bytes 524320 | tf_op jit(solution)/shard_map/ppermute | solution.py:51
  19.1 2.3 %collective-permute-done.2.refs_6_ = bf16[64,4096]{1,0:T(8,128)(2,1)S(1)} collective-permute-done((bf16[64,4096]{1,0:T(8,128)(2,1)}, bf16[64,4096]{1,0:T(8,128)(2,1)S(1)}, u32[]{:S(2)}, u32[]{:S(2)}) %collective-permute-start.2) | collective-permute-done | bytes 524320 | tf_op jit(solution)/shard_map/ppermute | solution.py:51
  21.4 1.8 %collective-permute-start.10 = (bf16[64,4096]{1,0:T(8,128)(2,1)S(1)}, bf16[64,4096]{1,0:T(8,128)(2,1)S(1)}, u32[]{:S(2)}, u32[]{:S(2)}) collective-permute-start(bf16[64,4096]{1,0:T(8,128)(2,1)S(1)} %collective-permute-done.2.refs_6_), channel_id=1, source_target_pairs={{0,8},{8,0},{16,24},{24,16},{32,40},{40,32},{48,56},{56,48},{64,72... | collective-permute-start | bytes 1572872 | tf_op jit(solution)/shard_map/ppermute | solution.py:51
  23.8 2.7 %collective-permute-start.5 = (bf16[64,4096]{1,0:T(8,128)(2,1)}, bf16[64,4096]{1,0:T(8,128)(2,1)S(1)}, u32[]{:S(2)}, u32[]{:S(2)}) collective-permute-start(bf16[64,4096]{1,0:T(8,128)(2,1)} %collective-permute-done.1.refs_4_), channel_id=1, source_target_pairs={{0,112},{8,120},{16,0},{24,8},{32,16},{40,24},{48,32},{56,40},{64,... | collective-permute-start | bytes 1572872 | tf_op jit(solution)/shard_map/ppermute | solution.py:51
  26.5 0.8 copy-done.9
  27.3 2.9 %collective-permute-start.6 = (bf16[64,4096]{1,0:T(8,128)(2,1)}, bf16[64,4096]{1,0:T(8,128)(2,1)S(1)}, u32[]{:S(2)}, u32[]{:S(2)}) collective-permute-start(bf16[64,4096]{1,0:T(8,128)(2,1)} %collective-permute-done.1.refs_4_), channel_id=1, source_target_pairs={{0,128},{8,136},{16,144},{24,152},{32,160},{40,168},{48,176},{56,1... | collective-permute-start | bytes 1572872 | tf_op jit(solution)/shard_map/ppermute | solution.py:51
  30.2 5.3 %all-to-all-start = ((f32[16,64,128]{2,1,0:T(8,128)}), f32[16,64,128]{2,1,0:T(8,128)S(1)}, u32[]{:S(2)}, u32[]{:S(2)}) async-start(f32[16,64,128]{2,1,0:T(8,128)} %pack.1), calls=%async_computation | async-start | bytes 1048576 | tf_op jit(solution)/shard_map/all_to_all | solution.py:389
  35.7 2.9 %collective-permute-start.13 = (bf16[64,4096]{1,0:T(8,128)(2,1)}, bf16[64,4096]{1,0:T(8,128)(2,1)S(1)}, u32[]{:S(2)}, u32[]{:S(2)}) collective-permute-start(bf16[64,4096]{1,0:T(8,128)(2,1)} %collective-permute-done.refs_2_), channel_id=1, source_target_pairs={{0,128},{8,136},{16,144},{24,152},{32,160},{40,168},{48,176},{56,1... | collective-permute-start | bytes 1572872 | tf_op jit(solution)/shard_map/ppermute | solution.py:51
  38.5 6.3 %grad_columns.3.refs_8_ = bf16[448,2048]{1,0:T(8,128)(2,1)} custom-call(s32[5]{0:T(128)S(1)} %stack.88.place_ref, bf16[448,4096]{1,0:T(8,128)(2,1)} %weight_hbm.7, bf16[64,4096]{1,0:T(8,128)(2,1)} %bitcast.35, bf16[64,4096]{1,0:T(8,128)(2,1)} %copy-done.8, bf16[64,4096]{1,0:T(8,128)(2,1)} %collective-permute-done.refs_2_, ...), custom_call_target="tpu_custom_call" | custom-call | tf_op jit(solution)/shard_map/grad_columns/pallas_call | solution.py:57
  44.9 1.3 %collective-permute-start.11 = (bf16[64,4096]{1,0:T(8,128)(2,1)S(1)}, bf16[64,4096]{1,0:T(8,128)(2,1)}, u32[]{:S(2)}, u32[]{:S(2)}) collective-permute-start(bf16[64,4096]{1,0:T(8,128)(2,1)S(1)} %collective-permute-done.4.refs_0_), channel_id=1, source_target_pairs={{0,16},{8,24},{16,32},{24,40},{32,48},{40,56},{48,64},{56,72},{64,... | collective-permute-start | bytes 1572872 | tf_op jit(solution)/shard_map/ppermute | solution.py:51
  46.1 1.5 %collective-permute-start.12 = (bf16[64,4096]{1,0:T(8,128)(2,1)S(1)}, bf16[64,4096]{1,0:T(8,128)(2,1)}, u32[]{:S(2)}, u32[]{:S(2)}) collective-permute-start(bf16[64,4096]{1,0:T(8,128)(2,1)S(1)} %collective-permute-done.5.refs_2_), channel_id=1, source_target_pairs={{0,112},{8,120},{16,0},{24,8},{32,16},{40,24},{48,32},{56,40},{64,... | collective-permute-start | bytes 1572872 | tf_op jit(solution)/shard_map/ppermute | solution.py:51
  47.6 3.4 %all-to-all-done.packed_ref = f32[16,64,128]{2,1,0:T(8,128)S(1)} async-done(((f32[16,64,128]{2,1,0:T(8,128)}), f32[16,64,128]{2,1,0:T(8,128)S(1)}, u32[]{:S(2)}, u32[]{:S(2)}) %all-to-all-start) | async-done | bytes 524320 | tf_op jit(solution)/shard_map/all_to_all | solution.py:389
  51.1 0.6 left.1.left_ref
  51.7 4.8 %collective-permute-start.14 = (f32[32,128]{1,0:T(8,128)S(1)}, f32[32,128]{1,0:T(8,128)S(1)}, u32[]{:S(2)}, u32[]{:S(2)}) collective-permute-start(f32[32,128]{1,0:T(8,128)S(1)} %left.1.left_ref), channel_id=1, source_target_pairs={{0,8},{8,0},{16,24},{24,16},{32,40},{40,32},{48,56},{56,48},{64,72... | collective-permute-start | bytes 49160 | tf_op jit(solution)/shard_map/ppermute | solution.py:51
  57.6 1.6 %feats.1 = f32[16,8,128]{2,1,0:T(8,128)} custom-call(s32[3]{0:T(128)S(1)} %pad_add_fusion.info_ref, f32[16,64,128]{2,1,0:T(8,128)S(1)} %all-to-all-done.packed_ref, f32[32,128]{1,0:T(8,128)S(1)} %left.1.left_ref, f32[32,128]{1,0:T(8,128)S(1)} %collective-permute-done.14.other_ref, s32[1,2048]{1,0:T(1,128)S(1)} %copy-done), custom_call_target="tpu_custom_call" | custom-call | tf_op jit(solution)/shard_map/feats/pallas_call | solution.py:57
  59.2 1.0 collective-permute-start.20
  60.2 0.9 collective-permute-done.11.refs_6_
  61.1 1.4 %collective-permute-start.21 = (bf16[64,4096]{1,0:T(8,128)(2,1)}, bf16[64,4096]{1,0:T(8,128)(2,1)S(1)}, u32[]{:S(2)}, u32[]{:S(2)}) collective-permute-start(bf16[64,4096]{1,0:T(8,128)(2,1)} %collective-permute-done.11.refs_6_), channel_id=1, source_target_pairs={{0,8},{8,0},{16,24},{24,16},{32,40},{40,32},{48,56},{56,48},{64,72... | collective-permute-start | bytes 1572872 | tf_op jit(solution)/shard_map/ppermute | solution.py:51
  62.5 2.7 %collective-permute-start.17 = (bf16[64,4096]{1,0:T(8,128)(2,1)S(1)}, bf16[64,4096]{1,0:T(8,128)(2,1)}, u32[]{:S(2)}, u32[]{:S(2)}) collective-permute-start(bf16[64,4096]{1,0:T(8,128)(2,1)S(1)} %collective-permute-done.5.refs_2_), channel_id=1, source_target_pairs={{0,128},{8,136},{16,144},{24,152},{32,160},{40,168},{48,176},{56,1... | collective-permute-start | bytes 1572872 | tf_op jit(solution)/shard_map/ppermute | solution.py:51
  65.2 2.7 %collective-permute-start.16 = (bf16[64,4096]{1,0:T(8,128)(2,1)}, bf16[64,4096]{1,0:T(8,128)(2,1)}, u32[]{:S(2)}, u32[]{:S(2)}) collective-permute-start(bf16[64,4096]{1,0:T(8,128)(2,1)} %collective-permute-done.12.refs_0_), channel_id=1, source_target_pairs={{0,112},{8,120},{16,0},{24,8},{32,16},{40,24},{48,32},{56,40},{64,... | collective-permute-start | bytes 1572872 | tf_op jit(solution)/shard_map/ppermute | solution.py:51
  67.9 0.8 collective-permute-start.25
  68.8 0.8 copy-done.16
  69.5 0.8 collective-permute-start.26
  70.3 5.1 %all-to-all-start.1 = ((f32[16,8,128]{2,1,0:T(8,128)}), f32[16,8,128]{2,1,0:T(8,128)S(1)}, u32[]{:S(2)}, u32[]{:S(2)}) async-start(f32[16,8,128]{2,1,0:T(8,128)} %feats.1), calls=%async_computation.1 | async-start | bytes 131072 | tf_op jit(solution)/shard_map/all_to_all | solution.py:412
  75.6 6.3 %grad_columns.4.refs_8_ = bf16[448,2048]{1,0:T(8,128)(2,1)} custom-call(s32[5]{0:T(128)S(1)} %stack.93.place_ref, bf16[448,4096]{1,0:T(8,128)(2,1)} %weight_hbm.7, bf16[64,4096]{1,0:T(8,128)(2,1)} %copy-done.3, bf16[64,4096]{1,0:T(8,128)(2,1)} %copy-done.13, bf16[64,4096]{1,0:T(8,128)(2,1)} %copy-done.2, ...), custom_call_target="tpu_custom_call", output_to_operand_aliasing={{}: (10, {})} | custom-call | tf_op jit(solution)/shard_map/grad_columns/pallas_call | solution.py:57
  81.9 2.5 %all-to-all-done.1 = f32[16,8,128]{2,1,0:T(8,128)S(1)} async-done(((f32[16,8,128]{2,1,0:T(8,128)}), f32[16,8,128]{2,1,0:T(8,128)S(1)}, u32[]{:S(2)}, u32[]{:S(2)}) %all-to-all-start.1) | async-done | bytes 65568 | tf_op jit(solution)/shard_map/all_to_all | solution.py:412
  84.5 1.3 %collective-permute-start.27 = (bf16[64,4096]{1,0:T(8,128)(2,1)}, bf16[64,4096]{1,0:T(8,128)(2,1)}, u32[]{:S(2)}, u32[]{:S(2)}) collective-permute-start(bf16[64,4096]{1,0:T(8,128)(2,1)} %collective-permute-done.15.refs_4_), channel_id=1, source_target_pairs={{0,8},{8,0},{16,24},{24,16},{32,40},{40,32},{48,56},{56,48},{64,72... | collective-permute-start | bytes 1572872 | tf_op jit(solution)/shard_map/ppermute | solution.py:51
  85.9 0.7 collective-permute-start.22
  86.6 2.0 %collective-permute-start.23 = (bf16[64,4096]{1,0:T(8,128)(2,1)}, bf16[64,4096]{1,0:T(8,128)(2,1)S(1)}, u32[]{:S(2)}, u32[]{:S(2)}) collective-permute-start(bf16[64,4096]{1,0:T(8,128)(2,1)} %collective-permute-done.17.refs_0_), channel_id=1, source_target_pairs={{0,112},{8,120},{16,0},{24,8},{32,16},{40,24},{48,32},{56,40},{64,... | collective-permute-start | bytes 1572872 | tf_op jit(solution)/shard_map/ppermute | solution.py:51
  88.6 1.6 %collective-permute-start.24 = (bf16[64,4096]{1,0:T(8,128)(2,1)}, bf16[64,4096]{1,0:T(8,128)(2,1)S(1)}, u32[]{:S(2)}, u32[]{:S(2)}) collective-permute-start(bf16[64,4096]{1,0:T(8,128)(2,1)} %collective-permute-done.16.refs_6_), channel_id=1, source_target_pairs={{0,128},{8,136},{16,144},{24,152},{32,160},{40,168},{48,176},{56,1... | collective-permute-start | bytes 1572872 | tf_op jit(solution)/shard_map/ppermute | solution.py:51
  90.2 0.8 broadcast_in_dim.11
  91.0 4.1 %all-to-all-start.2 = ((f32[8,128,128]{2,1,0:T(8,128)}), f32[8,128,128]{2,1,0:T(8,128)S(1)}, u32[]{:S(2)}, u32[]{:S(2)}) async-start(f32[8,128,128]{2,1,0:T(8,128)} %broadcast_in_dim.11), calls=%async_computation.2 | async-start | bytes 1048576 | tf_op jit(solution)/shard_map/all_to_all | solution.py:421
  95.2 1.6 %collective-permute-start.30 = (bf16[64,4096]{1,0:T(8,128)(2,1)}, bf16[64,4096]{1,0:T(8,128)(2,1)S(1)}, u32[]{:S(2)}, u32[]{:S(2)}) collective-permute-start(bf16[64,4096]{1,0:T(8,128)(2,1)} %collective-permute-done.17.refs_0_), channel_id=1, source_target_pairs={{0,8},{8,0},{16,24},{24,16},{32,40},{40,32},{48,56},{56,48},{64,72... | collective-permute-start | bytes 1572872 | tf_op jit(solution)/shard_map/ppermute | solution.py:51
  96.8 6.3 %grad_columns.5.refs_8_ = bf16[448,2048]{1,0:T(8,128)(2,1)} custom-call(s32[5]{0:T(128)S(1)} %stack.98.place_ref, bf16[448,4096]{1,0:T(8,128)(2,1)} %weight_hbm.7, bf16[64,4096]{1,0:T(8,128)(2,1)} %collective-permute-done.12.refs_0_, bf16[64,4096]{1,0:T(8,128)(2,1)} %copy-done.7, bf16[64,4096]{1,0:T(8,128)(2,1)} %copy-done.5, ...), custom_call_target="tpu_custom_call", output_to_operand_aliasing={{}: (10, {})} | custom-call | tf_op jit(solution)/shard_map/grad_columns/pallas_call | solution.py:57
  103.0 4.3 %all-to-all-done.2.mine_ref = f32[8,128,128]{2,1,0:T(8,128)S(1)} async-done(((f32[8,128,128]{2,1,0:T(8,128)}), f32[8,128,128]{2,1,0:T(8,128)S(1)}, u32[]{:S(2)}, u32[]{:S(2)}) %all-to-all-start.2) | async-done | bytes 524320 | tf_op jit(solution)/shard_map/all_to_all | solution.py:421
  107.4 2.1 %collective-permute-start.29 = (f32[8,128,128]{2,1,0:T(8,128)S(1)}, f32[8,128,128]{2,1,0:T(8,128)S(1)}, u32[]{:S(2)}, u32[]{:S(2)}) collective-permute-start(f32[8,128,128]{2,1,0:T(8,128)S(1)} %all-to-all-done.2.mine_ref), channel_id=1, source_target_pairs={{0,8},{8,0},{16,24},{24,16},{32,40},{40,32},{48,56},{56,48},{64,72... | collective-permute-start | bytes 1572872 | tf_op jit(solution)/shard_map/ppermute | solution.py:51
  110.3 0.8 collective-permute-done.29.other_ref
  111.1 0.9 collective-permute-done.31.refs_3_
  112.0 0.7 collective-permute-done.32.refs_5_
  112.7 0.7 collective-permute-done.33.refs_7_
  113.5 10.9 %finish.1 = (bf16[448,2048]{1,0:T(8,128)(2,1)}, f32[512,128]{1,0:T(8,128)}, f32[1,64]{1,0:T(1,128)}) custom-call(s32[3]{0:T(128)S(1)} %pad_add_fusion.info_ref, s32[4]{0:T(128)S(1)} %pad_add_fusion.1.place_ref, f32[8,128,128]{2,1,0:T(8,128)S(1)} %all-to-all-done.2.mine_ref, ...), custom_call_target="tpu_custom_call", output_to_operand_aliasing={{0}: (13, {})} | custom-call | tf_op jit(solution)/shard_map/finish/pallas_call | solution.py:57
  (76 shorter events, 3.1 us)
Async XLA Ops:
  0.6 14.0 %copy-start.1 = (bf16[1,64,4096]{2,1,0:T(8,128)(2,1)S(1)}, bf16[1,64,4096]{2,1,0:T(8,128)(2,1)}, u32[]{:S(2)}) copy-start(bf16[1,64,4096]{2,1,0:T(8,128)(2,1)} %param.7) | copy-start | bytes 1572868
  0.6 18.5 %collective-permute-start = (bf16[64,4096]{1,0:T(8,128)(2,1)}, bf16[64,4096]{1,0:T(8,128)(2,1)}, u32[]{:S(2)}, u32[]{:S(2)}) collective-permute-start(bf16[64,4096]{1,0:T(8,128)(2,1)} %bitcast.31), channel_id=1, source_target_pairs={{0,16},{8,24},{16,32},{24,40},{32,48},{40,56},{48,64},{56,72},{64,... | collective-permute-start | bytes 1572872 | tf_op jit(solution)/shard_map/ppermute | solution.py:51
  3.2 15.9 %collective-permute-start.1 = (bf16[64,4096]{1,0:T(8,128)(2,1)}, bf16[64,4096]{1,0:T(8,128)(2,1)}, u32[]{:S(2)}, u32[]{:S(2)}) collective-permute-start(bf16[64,4096]{1,0:T(8,128)(2,1)} %bitcast.32), channel_id=1, source_target_pairs={{0,112},{8,120},{16,0},{24,8},{32,16},{40,24},{48,32},{56,40},{64,... | collective-permute-start | bytes 1572872 | tf_op jit(solution)/shard_map/ppermute | solution.py:51
  7.2 14.2 %collective-permute-start.2 = (bf16[64,4096]{1,0:T(8,128)(2,1)}, bf16[64,4096]{1,0:T(8,128)(2,1)S(1)}, u32[]{:S(2)}, u32[]{:S(2)}) collective-permute-start(bf16[64,4096]{1,0:T(8,128)(2,1)} %bitcast.33), channel_id=1, source_target_pairs={{0,128},{8,136},{16,144},{24,152},{32,160},{40,168},{48,176},{56,1... | collective-permute-start | bytes 1572872 | tf_op jit(solution)/shard_map/ppermute | solution.py:51
  13.3 2.5 %collective-permute-start.3 = (f32[32,2176]{1,0:T(8,128)S(1)}, f32[32,2176]{1,0:T(8,128)S(1)}, u32[]{:S(2)}, u32[]{:S(2)}) collective-permute-start(f32[32,2176]{1,0:T(8,128)S(1)} %get-tuple-element.31), channel_id=1, source_target_pairs={{0,8},{8,0},{16,24},{24,16},{32,40},{40,32},{48,56},{56,48},{64,72... | collective-permute-start | bytes 835592 | tf_op jit(solution)/shard_map/ppermute | solution.py:51
  14.6 9.2 %collective-permute-start.7 = (bf16[64,4096]{1,0:T(8,128)(2,1)S(1)}, bf16[64,4096]{1,0:T(8,128)(2,1)S(1)}, u32[]{:S(2)}, u32[]{:S(2)}) collective-permute-start(bf16[64,4096]{1,0:T(8,128)(2,1)S(1)} %bitcast.36), channel_id=1, source_target_pairs={{0,8},{8,0},{16,24},{24,16},{32,40},{40,32},{48,56},{56,48},{64,72... | collective-permute-start | bytes 1572872 | tf_op jit(solution)/shard_map/ppermute | solution.py:51
  21.4 8.7 %copy-start.6 = (bf16[64,4096]{1,0:T(8,128)(2,1)}, bf16[64,4096]{1,0:T(8,128)(2,1)S(1)}, u32[]{:S(2)}) copy-start(bf16[64,4096]{1,0:T(8,128)(2,1)S(1)} %collective-permute-done.2.refs_6_) | copy-start | bytes 1572868
  21.4 5.0 %collective-permute-start.10 = (bf16[64,4096]{1,0:T(8,128)(2,1)S(1)}, bf16[64,4096]{1,0:T(8,128)(2,1)S(1)}, u32[]{:S(2)}, u32[]{:S(2)}) collective-permute-start(bf16[64,4096]{1,0:T(8,128)(2,1)S(1)} %collective-permute-done.2.refs_6_), channel_id=1, source_target_pairs={{0,8},{8,0},{16,24},{24,16},{32,40},{40,32},{48,56},{56,48},{64,72... | collective-permute-start | bytes 1572872 | tf_op jit(solution)/shard_map/ppermute | solution.py:51
  23.3 12.4 %collective-permute-start.8 = (bf16[64,4096]{1,0:T(8,128)(2,1)}, bf16[64,4096]{1,0:T(8,128)(2,1)}, u32[]{:S(2)}, u32[]{:S(2)}) collective-permute-start(bf16[64,4096]{1,0:T(8,128)(2,1)} %collective-permute-done.refs_2_), channel_id=1, source_target_pairs={{0,8},{8,0},{16,24},{24,16},{32,40},{40,32},{48,56},{56,48},{64,72... | collective-permute-start | bytes 1572872 | tf_op jit(solution)/shard_map/ppermute | solution.py:51
  23.3 15.3 %collective-permute-start.9 = (bf16[64,4096]{1,0:T(8,128)(2,1)}, bf16[64,4096]{1,0:T(8,128)(2,1)}, u32[]{:S(2)}, u32[]{:S(2)}) collective-permute-start(bf16[64,4096]{1,0:T(8,128)(2,1)} %collective-permute-done.1.refs_4_), channel_id=1, source_target_pairs={{0,8},{8,0},{16,24},{24,16},{32,40},{40,32},{48,56},{56,48},{64,72... | collective-permute-start | bytes 1572872 | tf_op jit(solution)/shard_map/ppermute | solution.py:51
  23.8 21.0 %collective-permute-start.4 = (bf16[64,4096]{1,0:T(8,128)(2,1)}, bf16[64,4096]{1,0:T(8,128)(2,1)S(1)}, u32[]{:S(2)}, u32[]{:S(2)}) collective-permute-start(bf16[64,4096]{1,0:T(8,128)(2,1)} %collective-permute-done.refs_2_), channel_id=1, source_target_pairs={{0,16},{8,24},{16,32},{24,40},{32,48},{40,56},{48,64},{56,72},{64,... | collective-permute-start | bytes 1572872 | tf_op jit(solution)/shard_map/ppermute | solution.py:51
  23.8 11.8 %copy-start.8 = (bf16[64,4096]{1,0:T(8,128)(2,1)}, bf16[64,4096]{1,0:T(8,128)(2,1)S(1)}, u32[]{:S(2)}) copy-start(bf16[64,4096]{1,0:T(8,128)(2,1)S(1)} %collective-permute-done.7.refs_1_) | copy-start | bytes 1572868
  23.8 21.0 %collective-permute-start.5 = (bf16[64,4096]{1,0:T(8,128)(2,1)}, bf16[64,4096]{1,0:T(8,128)(2,1)S(1)}, u32[]{:S(2)}, u32[]{:S(2)}) collective-permute-start(bf16[64,4096]{1,0:T(8,128)(2,1)} %collective-permute-done.1.refs_4_), channel_id=1, source_target_pairs={{0,112},{8,120},{16,0},{24,8},{32,16},{40,24},{48,32},{56,40},{64,... | collective-permute-start | bytes 1572872 | tf_op jit(solution)/shard_map/ppermute | solution.py:51
  27.3 17.6 %collective-permute-start.6 = (bf16[64,4096]{1,0:T(8,128)(2,1)}, bf16[64,4096]{1,0:T(8,128)(2,1)S(1)}, u32[]{:S(2)}, u32[]{:S(2)}) collective-permute-start(bf16[64,4096]{1,0:T(8,128)(2,1)} %collective-permute-done.1.refs_4_), channel_id=1, source_target_pairs={{0,128},{8,136},{16,144},{24,152},{32,160},{40,168},{48,176},{56,1... | collective-permute-start | bytes 1572872 | tf_op jit(solution)/shard_map/ppermute | solution.py:51
  30.2 20.9 %all-to-all-start = ((f32[16,64,128]{2,1,0:T(8,128)}), f32[16,64,128]{2,1,0:T(8,128)S(1)}, u32[]{:S(2)}, u32[]{:S(2)}) async-start(f32[16,64,128]{2,1,0:T(8,128)} %pack.1), calls=%async_computation | async-start | bytes 1048576 | tf_op jit(solution)/shard_map/all_to_all | solution.py:389
  35.7 21.9 %copy-start = (s32[1,2048]{1,0:T(1,128)S(1)}, s32[1,2048]{1,0:T(1,128)}, u32[]{:S(2)}) copy-start(s32[1,2048]{1,0:T(1,128)} %ids_ref.1) | copy-start | bytes 24580
  35.7 23.5 %collective-permute-start.13 = (bf16[64,4096]{1,0:T(8,128)(2,1)}, bf16[64,4096]{1,0:T(8,128)(2,1)S(1)}, u32[]{:S(2)}, u32[]{:S(2)}) collective-permute-start(bf16[64,4096]{1,0:T(8,128)(2,1)} %collective-permute-done.refs_2_), channel_id=1, source_target_pairs={{0,128},{8,136},{16,144},{24,152},{32,160},{40,168},{48,176},{56,1... | collective-permute-start | bytes 1572872 | tf_op jit(solution)/shard_map/ppermute | solution.py:51
  44.8 30.8 %copy-start.3 = (bf16[64,4096]{1,0:T(8,128)(2,1)}, bf16[64,4096]{1,0:T(8,128)(2,1)S(1)}, u32[]{:S(2)}) copy-start(bf16[64,4096]{1,0:T(8,128)(2,1)S(1)} %collective-permute-done.4.refs_0_) | copy-start | bytes 1572868
  44.9 30.8 %copy-start.2 = (bf16[64,4096]{1,0:T(8,128)(2,1)}, bf16[64,4096]{1,0:T(8,128)(2,1)S(1)}, u32[]{:S(2)}) copy-start(bf16[64,4096]{1,0:T(8,128)(2,1)S(1)} %collective-permute-done.5.refs_2_) | copy-start | bytes 1572868
  44.9 30.7 %copy-start.4 = (bf16[64,4096]{1,0:T(8,128)(2,1)}, bf16[64,4096]{1,0:T(8,128)(2,1)S(1)}, u32[]{:S(2)}) copy-start(bf16[64,4096]{1,0:T(8,128)(2,1)S(1)} %collective-permute-done.6.refs_4_) | copy-start | bytes 1572868
  44.9 16.2 %collective-permute-start.11 = (bf16[64,4096]{1,0:T(8,128)(2,1)S(1)}, bf16[64,4096]{1,0:T(8,128)(2,1)}, u32[]{:S(2)}, u32[]{:S(2)}) collective-permute-start(bf16[64,4096]{1,0:T(8,128)(2,1)S(1)} %collective-permute-done.4.refs_0_), channel_id=1, source_target_pairs={{0,16},{8,24},{16,32},{24,40},{32,48},{40,56},{48,64},{56,72},{64,... | collective-permute-start | bytes 1572872 | tf_op jit(solution)/shard_map/ppermute | solution.py:51
  46.1 14.9 %collective-permute-start.12 = (bf16[64,4096]{1,0:T(8,128)(2,1)S(1)}, bf16[64,4096]{1,0:T(8,128)(2,1)}, u32[]{:S(2)}, u32[]{:S(2)}) collective-permute-start(bf16[64,4096]{1,0:T(8,128)(2,1)S(1)} %collective-permute-done.5.refs_2_), channel_id=1, source_target_pairs={{0,112},{8,120},{16,0},{24,8},{32,16},{40,24},{48,32},{56,40},{64,... | collective-permute-start | bytes 1572872 | tf_op jit(solution)/shard_map/ppermute | solution.py:51
  51.7 5.6 %collective-permute-start.14 = (f32[32,128]{1,0:T(8,128)S(1)}, f32[32,128]{1,0:T(8,128)S(1)}, u32[]{:S(2)}, u32[]{:S(2)}) collective-permute-start(f32[32,128]{1,0:T(8,128)S(1)} %left.1.left_ref), channel_id=1, source_target_pairs={{0,8},{8,0},{16,24},{24,16},{32,40},{40,32},{48,56},{56,48},{64,72... | collective-permute-start | bytes 49160 | tf_op jit(solution)/shard_map/ppermute | solution.py:51
  56.4 8.8 %collective-permute-start.18 = (bf16[64,4096]{1,0:T(8,128)(2,1)S(1)}, bf16[64,4096]{1,0:T(8,128)(2,1)S(1)}, u32[]{:S(2)}, u32[]{:S(2)}) collective-permute-start(bf16[64,4096]{1,0:T(8,128)(2,1)S(1)} %collective-permute-done.4.refs_0_), channel_id=1, source_target_pairs={{0,8},{8,0},{16,24},{24,16},{32,40},{40,32},{48,56},{56,48},{64,72... | collective-permute-start | bytes 1572872 | tf_op jit(solution)/shard_map/ppermute | solution.py:51
  57.2 8.0 %collective-permute-start.19 = (bf16[64,4096]{1,0:T(8,128)(2,1)S(1)}, bf16[64,4096]{1,0:T(8,128)(2,1)S(1)}, u32[]{:S(2)}, u32[]{:S(2)}) collective-permute-start(bf16[64,4096]{1,0:T(8,128)(2,1)S(1)} %collective-permute-done.5.refs_2_), channel_id=1, source_target_pairs={{0,8},{8,0},{16,24},{24,16},{32,40},{40,32},{48,56},{56,48},{64,72... | collective-permute-start | bytes 1572872 | tf_op jit(solution)/shard_map/ppermute | solution.py:51
  59.2 22.7 %copy-start.5 = (bf16[64,4096]{1,0:T(8,128)(2,1)}, bf16[64,4096]{1,0:T(8,128)(2,1)S(1)}, u32[]{:S(2)}) copy-start(bf16[64,4096]{1,0:T(8,128)(2,1)S(1)} %collective-permute-done.13.refs_2_) | copy-start | bytes 1572868
  59.2 8.7 %collective-permute-start.20 = (bf16[64,4096]{1,0:T(8,128)(2,1)S(1)}, bf16[64,4096]{1,0:T(8,128)(2,1)S(1)}, u32[]{:S(2)}, u32[]{:S(2)}) collective-permute-start(bf16[64,4096]{1,0:T(8,128)(2,1)S(1)} %collective-permute-done.6.refs_4_), channel_id=1, source_target_pairs={{0,8},{8,0},{16,24},{24,16},{32,40},{40,32},{48,56},{56,48},{64,72... | collective-permute-start | bytes 1572872 | tf_op jit(solution)/shard_map/ppermute | solution.py:51
  61.1 7.6 %collective-permute-start.21 = (bf16[64,4096]{1,0:T(8,128)(2,1)}, bf16[64,4096]{1,0:T(8,128)(2,1)S(1)}, u32[]{:S(2)}, u32[]{:S(2)}) collective-permute-start(bf16[64,4096]{1,0:T(8,128)(2,1)} %collective-permute-done.11.refs_6_), channel_id=1, source_target_pairs={{0,8},{8,0},{16,24},{24,16},{32,40},{40,32},{48,56},{56,48},{64,72... | collective-permute-start | bytes 1572872 | tf_op jit(solution)/shard_map/ppermute | solution.py:51
  62.5 19.4 %collective-permute-start.17 = (bf16[64,4096]{1,0:T(8,128)(2,1)S(1)}, bf16[64,4096]{1,0:T(8,128)(2,1)}, u32[]{:S(2)}, u32[]{:S(2)}) collective-permute-start(bf16[64,4096]{1,0:T(8,128)(2,1)S(1)} %collective-permute-done.5.refs_2_), channel_id=1, source_target_pairs={{0,128},{8,136},{16,144},{24,152},{32,160},{40,168},{48,176},{56,1... | collective-permute-start | bytes 1572872 | tf_op jit(solution)/shard_map/ppermute | solution.py:51
  65.2 19.3 %collective-permute-start.15 = (bf16[64,4096]{1,0:T(8,128)(2,1)S(1)}, bf16[64,4096]{1,0:T(8,128)(2,1)}, u32[]{:S(2)}, u32[]{:S(2)}) collective-permute-start(bf16[64,4096]{1,0:T(8,128)(2,1)S(1)} %collective-permute-done.13.refs_2_), channel_id=1, source_target_pairs={{0,16},{8,24},{16,32},{24,40},{32,48},{40,56},{48,64},{56,72},{64,... | collective-permute-start | bytes 1572872 | tf_op jit(solution)/shard_map/ppermute | solution.py:51
  65.2 19.2 %collective-permute-start.16 = (bf16[64,4096]{1,0:T(8,128)(2,1)}, bf16[64,4096]{1,0:T(8,128)(2,1)}, u32[]{:S(2)}, u32[]{:S(2)}) collective-permute-start(bf16[64,4096]{1,0:T(8,128)(2,1)} %collective-permute-done.12.refs_0_), channel_id=1, source_target_pairs={{0,112},{8,120},{16,0},{24,8},{32,16},{40,24},{48,32},{56,40},{64,... | collective-permute-start | bytes 1572872 | tf_op jit(solution)/shard_map/ppermute | solution.py:51
  67.9 18.7 %collective-permute-start.25 = (bf16[64,4096]{1,0:T(8,128)(2,1)}, bf16[64,4096]{1,0:T(8,128)(2,1)S(1)}, u32[]{:S(2)}, u32[]{:S(2)}) collective-permute-start(bf16[64,4096]{1,0:T(8,128)(2,1)} %collective-permute-done.12.refs_0_), channel_id=1, source_target_pairs={{0,8},{8,0},{16,24},{24,16},{32,40},{40,32},{48,56},{56,48},{64,72... | collective-permute-start | bytes 1572872 | tf_op jit(solution)/shard_map/ppermute | solution.py:51
  69.5 19.0 %collective-permute-start.26 = (bf16[64,4096]{1,0:T(8,128)(2,1)S(1)}, bf16[64,4096]{1,0:T(8,128)(2,1)}, u32[]{:S(2)}, u32[]{:S(2)}) collective-permute-start(bf16[64,4096]{1,0:T(8,128)(2,1)S(1)} %collective-permute-done.13.refs_2_), channel_id=1, source_target_pairs={{0,8},{8,0},{16,24},{24,16},{32,40},{40,32},{48,56},{56,48},{64,72... | collective-permute-start | bytes 1572872 | tf_op jit(solution)/shard_map/ppermute | solution.py:51
  70.3 14.1 %all-to-all-start.1 = ((f32[16,8,128]{2,1,0:T(8,128)}), f32[16,8,128]{2,1,0:T(8,128)S(1)}, u32[]{:S(2)}, u32[]{:S(2)}) async-start(f32[16,8,128]{2,1,0:T(8,128)} %feats.1), calls=%async_computation.1 | async-start | bytes 131072 | tf_op jit(solution)/shard_map/all_to_all | solution.py:412
  84.5 10.8 %collective-permute-start.27 = (bf16[64,4096]{1,0:T(8,128)(2,1)}, bf16[64,4096]{1,0:T(8,128)(2,1)}, u32[]{:S(2)}, u32[]{:S(2)}) collective-permute-start(bf16[64,4096]{1,0:T(8,128)(2,1)} %collective-permute-done.15.refs_4_), channel_id=1, source_target_pairs={{0,8},{8,0},{16,24},{24,16},{32,40},{40,32},{48,56},{56,48},{64,72... | collective-permute-start | bytes 1572872 | tf_op jit(solution)/shard_map/ppermute | solution.py:51
  85.8 11.0 %collective-permute-start.28 = (bf16[64,4096]{1,0:T(8,128)(2,1)}, bf16[64,4096]{1,0:T(8,128)(2,1)}, u32[]{:S(2)}, u32[]{:S(2)}) collective-permute-start(bf16[64,4096]{1,0:T(8,128)(2,1)} %collective-permute-done.16.refs_6_), channel_id=1, source_target_pairs={{0,8},{8,0},{16,24},{24,16},{32,40},{40,32},{48,56},{56,48},{64,72... | collective-permute-start | bytes 1572872 | tf_op jit(solution)/shard_map/ppermute | solution.py:51
  85.9 21.5 %collective-permute-start.22 = (bf16[64,4096]{1,0:T(8,128)(2,1)}, bf16[64,4096]{1,0:T(8,128)(2,1)S(1)}, u32[]{:S(2)}, u32[]{:S(2)}) collective-permute-start(bf16[64,4096]{1,0:T(8,128)(2,1)} %collective-permute-done.15.refs_4_), channel_id=1, source_target_pairs={{0,16},{8,24},{16,32},{24,40},{32,48},{40,56},{48,64},{56,72},{64,... | collective-permute-start | bytes 1572872 | tf_op jit(solution)/shard_map/ppermute | solution.py:51
  86.6 20.8 %collective-permute-start.23 = (bf16[64,4096]{1,0:T(8,128)(2,1)}, bf16[64,4096]{1,0:T(8,128)(2,1)S(1)}, u32[]{:S(2)}, u32[]{:S(2)}) collective-permute-start(bf16[64,4096]{1,0:T(8,128)(2,1)} %collective-permute-done.17.refs_0_), channel_id=1, source_target_pairs={{0,112},{8,120},{16,0},{24,8},{32,16},{40,24},{48,32},{56,40},{64,... | collective-permute-start | bytes 1572872 | tf_op jit(solution)/shard_map/ppermute | solution.py:51
  88.6 18.8 %collective-permute-start.24 = (bf16[64,4096]{1,0:T(8,128)(2,1)}, bf16[64,4096]{1,0:T(8,128)(2,1)S(1)}, u32[]{:S(2)}, u32[]{:S(2)}) collective-permute-start(bf16[64,4096]{1,0:T(8,128)(2,1)} %collective-permute-done.16.refs_6_), channel_id=1, source_target_pairs={{0,128},{8,136},{16,144},{24,152},{32,160},{40,168},{48,176},{56,1... | collective-permute-start | bytes 1572872 | tf_op jit(solution)/shard_map/ppermute | solution.py:51
  91.0 16.4 %all-to-all-start.2 = ((f32[8,128,128]{2,1,0:T(8,128)}), f32[8,128,128]{2,1,0:T(8,128)S(1)}, u32[]{:S(2)}, u32[]{:S(2)}) async-start(f32[8,128,128]{2,1,0:T(8,128)} %broadcast_in_dim.11), calls=%async_computation.2 | async-start | bytes 1048576 | tf_op jit(solution)/shard_map/all_to_all | solution.py:421
  95.2 15.1 %collective-permute-start.30 = (bf16[64,4096]{1,0:T(8,128)(2,1)}, bf16[64,4096]{1,0:T(8,128)(2,1)S(1)}, u32[]{:S(2)}, u32[]{:S(2)}) collective-permute-start(bf16[64,4096]{1,0:T(8,128)(2,1)} %collective-permute-done.17.refs_0_), channel_id=1, source_target_pairs={{0,8},{8,0},{16,24},{24,16},{32,40},{40,32},{48,56},{56,48},{64,72... | collective-permute-start | bytes 1572872 | tf_op jit(solution)/shard_map/ppermute | solution.py:51
  107.4 6.1 %copy-start.10 = (bf16[64,4096]{1,0:T(8,128)(2,1)}, bf16[64,4096]{1,0:T(8,128)(2,1)S(1)}, u32[]{:S(2)}) copy-start(bf16[64,4096]{1,0:T(8,128)(2,1)S(1)} %collective-permute-done.22.refs_2_) | copy-start | bytes 1572868
  107.4 6.1 %copy-start.11 = (bf16[64,4096]{1,0:T(8,128)(2,1)}, bf16[64,4096]{1,0:T(8,128)(2,1)S(1)}, u32[]{:S(2)}) copy-start(bf16[64,4096]{1,0:T(8,128)(2,1)S(1)} %collective-permute-done.23.refs_4_) | copy-start | bytes 1572868
  107.4 6.1 %copy-start.12 = (bf16[64,4096]{1,0:T(8,128)(2,1)}, bf16[64,4096]{1,0:T(8,128)(2,1)S(1)}, u32[]{:S(2)}) copy-start(bf16[64,4096]{1,0:T(8,128)(2,1)S(1)} %collective-permute-done.24.refs_6_) | copy-start | bytes 1572868
  107.4 3.7 %collective-permute-start.29 = (f32[8,128,128]{2,1,0:T(8,128)S(1)}, f32[8,128,128]{2,1,0:T(8,128)S(1)}, u32[]{:S(2)}, u32[]{:S(2)}) collective-permute-start(f32[8,128,128]{2,1,0:T(8,128)S(1)} %all-to-all-done.2.mine_ref), channel_id=1, source_target_pairs={{0,8},{8,0},{16,24},{24,16},{32,40},{40,32},{48,56},{56,48},{64,72... | collective-permute-start | bytes 1572872 | tf_op jit(solution)/shard_map/ppermute | solution.py:51
  109.5 2.4 %collective-permute-start.31 = (bf16[64,4096]{1,0:T(8,128)(2,1)S(1)}, bf16[64,4096]{1,0:T(8,128)(2,1)}, u32[]{:S(2)}, u32[]{:S(2)}) collective-permute-start(bf16[64,4096]{1,0:T(8,128)(2,1)S(1)} %collective-permute-done.22.refs_2_), channel_id=1, source_target_pairs={{0,8},{8,0},{16,24},{24,16},{32,40},{40,32},{48,56},{56,48},{64,72... | collective-permute-start | bytes 1572872 | tf_op jit(solution)/shard_map/ppermute | solution.py:51
  109.7 3.0 %collective-permute-start.32 = (bf16[64,4096]{1,0:T(8,128)(2,1)S(1)}, bf16[64,4096]{1,0:T(8,128)(2,1)}, u32[]{:S(2)}, u32[]{:S(2)}) collective-permute-start(bf16[64,4096]{1,0:T(8,128)(2,1)S(1)} %collective-permute-done.23.refs_4_), channel_id=1, source_target_pairs={{0,8},{8,0},{16,24},{24,16},{32,40},{40,32},{48,56},{56,48},{64,72... | collective-permute-start | bytes 1572872 | tf_op jit(solution)/shard_map/ppermute | solution.py:51
  110.1 3.4 %collective-permute-start.33 = (bf16[64,4096]{1,0:T(8,128)(2,1)S(1)}, bf16[64,4096]{1,0:T(8,128)(2,1)}, u32[]{:S(2)}, u32[]{:S(2)}) collective-permute-start(bf16[64,4096]{1,0:T(8,128)(2,1)S(1)} %collective-permute-done.24.refs_6_), channel_id=1, source_target_pairs={{0,8},{8,0},{16,24},{24,16},{32,40},{40,32},{48,56},{56,48},{64,72... | collective-permute-start | bytes 1572872 | tf_op jit(solution)/shard_map/ppermute | solution.py:51
  (7 other events, 17.1 us)

commit v3 on v2

--- a/solution.py
+++ b/solution.py
@@ -264,7 +264,8 @@
         rows = slice(chip * EX_GRP, (chip + 1) * EX_GRP)
         for part, ref in enumerate((mine_ref, other_ref)):
             start = (part * CHIPS + chip) * LANES
-            full[:, start : start + LANES] = ref[:, rows, :].reshape(examples, LANES)
+            part_rows = ref[:, rows, :].reshape(examples, LANES)
+            full[:, start : start + LANES] = part_rows.astype(jnp.bfloat16)
 
     def columns(chip, upper):
         start = pl.multiple_of(chip * EX_GRP, EX_GRP)
@@ -288,7 +289,7 @@
         / examples
     )
     kernel = lax.dot_general(
-        full[...], full[...], NT, precision=EXACT, preferred_element_type=jnp.float32
+        full[...], full[...], NT, preferred_element_type=jnp.float32
     )
     sub = lax.broadcasted_iota(jnp.int32, kernel.shape, 0)
     lane = lax.broadcasted_iota(jnp.int32, kernel.shape, 1)
@@ -456,7 +457,7 @@
         ),
         args,
         [
-            pltpu.VMEM((examples, PROJ * PROJ), jnp.float32),
+            pltpu.VMEM((examples, PROJ * PROJ), jnp.bfloat16),
             pltpu.VMEM((width, depth), jnp.bfloat16),
             pltpu.VMEM((wide, depth), jnp.bfloat16),
             pltpu.VMEM((width, wide), jnp.float32),

time: 125 us -> 124 us (level)
  transfers between devices with their start and end apart: 37 -> 37, of which waited for: 12 -> 12; matrix products, arithmetic and copies ran while one was open for 1% -> 1% of each run, Pallas kernels for 20% -> 21%
where the time goes in v3:
time: 124 us
  starting transfers between devices  63.9 us (52%)
  Pallas kernels  35.7 us (29%)
  waiting for transfers between devices  20.2 us (16%)
  local copies, waits for them, and re-layouts  2.73 us (2%)
    ppermute x34, starting transfers between devices, permute(): return lax.ppermute(value, 'fsdp', pairs)  49.3 us
    pallas_call x8, Pallas kernels, call(): pl.pallas_call(kernel, name=name, out_shape=out_shape, in_specs=in_specs...  35.7 us
    ppermute x34, waiting for transfers between devices, permute(): return lax.ppermute(value, 'fsdp', pairs)  9.91 us
    all_to_all x1, starting transfers between devices, body(): lax.all_to_all(packed, 'fsdp', 0, 0, axis_index_groups=SAME_CORE, tiled=T...  5.3 us
    all_to_all x1, starting transfers between devices, body(): lax.all_to_all(feats, 'fsdp', 0, 0, axis_index_groups=SAME_CORE, tiled=True)  5.15 us
    all_to_all x1, waiting for transfers between devices, body(): lax.all_to_all(jnp.broadcast_to(feats.reshape(1, CHIPS * EX_GRP, LANES),...  4.32 us
    all_to_all x1, starting transfers between devices, body(): lax.all_to_all(jnp.broadcast_to(feats.reshape(1, CHIPS * EX_GRP, LANES),...  4.14 us
    all_to_all x1, waiting for transfers between devices, body(): lax.all_to_all(packed, 'fsdp', 0, 0, axis_index_groups=SAME_CORE, tiled=T...  3.44 us
  transfers between devices with their start and end apart: 37, of which 12 were waited for; matrix products, arithmetic and copies ran while one was open for 1% of the time, Pallas kernels for 21%

profile of v3, /device:TPU:1, one launch (start us, length us, event | category | flops | bytes accessed | tf_op | source)
XLA Modules:
  0.0 123.9 jit_solution(5806871093833503647)
XLA Ops:
  0.6 2.5 %collective-permute-start = (bf16[64,4096]{1,0:T(8,128)(2,1)}, bf16[64,4096]{1,0:T(8,128)(2,1)}, u32[]{:S(2)}, u32[]{:S(2)}) collective-permute-start(bf16[64,4096]{1,0:T(8,128)(2,1)} %bitcast.31), channel_id=1, source_target_pairs={{0,16},{8,24},{16,32},{24,40},{32,48},{40,56},{48,64},{56,72},{64,... | collective-permute-start | bytes 1572872 | tf_op jit(solution)/shard_map/ppermute | solution.py:51
  3.2 4.0 %collective-permute-start.1 = (bf16[64,4096]{1,0:T(8,128)(2,1)}, bf16[64,4096]{1,0:T(8,128)(2,1)}, u32[]{:S(2)}, u32[]{:S(2)}) collective-permute-start(bf16[64,4096]{1,0:T(8,128)(2,1)} %bitcast.32), channel_id=1, source_target_pairs={{0,112},{8,120},{16,0},{24,8},{32,16},{40,24},{48,32},{56,40},{64,... | collective-permute-start | bytes 1572872 | tf_op jit(solution)/shard_map/ppermute | solution.py:51
  7.2 2.9 %collective-permute-start.2 = (bf16[64,4096]{1,0:T(8,128)(2,1)}, bf16[64,4096]{1,0:T(8,128)(2,1)S(1)}, u32[]{:S(2)}, u32[]{:S(2)}) collective-permute-start(bf16[64,4096]{1,0:T(8,128)(2,1)} %bitcast.33), channel_id=1, source_target_pairs={{0,128},{8,136},{16,144},{24,152},{32,160},{40,168},{48,176},{56,1... | collective-permute-start | bytes 1572872 | tf_op jit(solution)/shard_map/ppermute | solution.py:51
  10.2 3.1 %project.1 = (f32[32,2176]{1,0:T(8,128)S(1)}, f32[32,2176]{1,0:T(8,128)S(1)}) custom-call(s32[3]{0:T(128)S(1)} %pad_add_fusion.info_ref, bf16[448,2048]{1,0:T(8,128)(2,1)} %bitcast.37, bf16[64,448]{1,0:T(8,128)(2,1)} %bitcast.40, bf16[64,4096]{1,0:T(8,128)(2,1)} %bitcast.34, bf16[64,4096]{1,0:T(8,128)(2,1)} %bitcast.38), custom_call_target="tpu_custom_call" | custom-call | tf_op jit(solution)/shard_map/project/pallas_call | solution.py:57
  13.3 1.3 %collective-permute-start.3 = (f32[32,2176]{1,0:T(8,128)S(1)}, f32[32,2176]{1,0:T(8,128)S(1)}, u32[]{:S(2)}, u32[]{:S(2)}) collective-permute-start(f32[32,2176]{1,0:T(8,128)S(1)} %get-tuple-element.31), channel_id=1, source_target_pairs={{0,8},{8,0},{16,24},{24,16},{32,40},{40,32},{48,56},{56,48},{64,72... | collective-permute-start | bytes 835592 | tf_op jit(solution)/shard_map/ppermute | solution.py:51
  14.7 1.1 collective-permute-done.3.taken_ref
  15.8 1.5 %pack.1 = f32[16,64,128]{2,1,0:T(8,128)} custom-call(s32[3]{0:T(128)S(1)} %pad_add_fusion.info_ref, f32[32,2176]{1,0:T(8,128)S(1)} %get-tuple-element.30.kept_ref, f32[32,2176]{1,0:T(8,128)S(1)} %collective-permute-done.3.taken_ref), custom_call_target="tpu_custom_call" | custom-call | tf_op jit(solution)/shard_map/pack/pallas_call | solution.py:57
  17.3 1.8 %collective-permute-done.refs_2_ = bf16[64,4096]{1,0:T(8,128)(2,1)} collective-permute-done((bf16[64,4096]{1,0:T(8,128)(2,1)}, bf16[64,4096]{1,0:T(8,128)(2,1)}, u32[]{:S(2)}, u32[]{:S(2)}) %collective-permute-start) | collective-permute-done | bytes 524320 | tf_op jit(solution)/shard_map/ppermute | solution.py:51
  19.1 2.3 %collective-permute-done.2.refs_6_ = bf16[64,4096]{1,0:T(8,128)(2,1)S(1)} collective-permute-done((bf16[64,4096]{1,0:T(8,128)(2,1)}, bf16[64,4096]{1,0:T(8,128)(2,1)S(1)}, u32[]{:S(2)}, u32[]{:S(2)}) %collective-permute-start.2) | collective-permute-done | bytes 524320 | tf_op jit(solution)/shard_map/ppermute | solution.py:51
  21.4 1.8 %collective-permute-start.10 = (bf16[64,4096]{1,0:T(8,128)(2,1)S(1)}, bf16[64,4096]{1,0:T(8,128)(2,1)S(1)}, u32[]{:S(2)}, u32[]{:S(2)}) collective-permute-start(bf16[64,4096]{1,0:T(8,128)(2,1)S(1)} %collective-permute-done.2.refs_6_), channel_id=1, source_target_pairs={{0,8},{8,0},{16,24},{24,16},{32,40},{40,32},{48,56},{56,48},{64,72... | collective-permute-start | bytes 1572872 | tf_op jit(solution)/shard_map/ppermute | solution.py:51
  23.8 2.7 %collective-permute-start.5 = (bf16[64,4096]{1,0:T(8,128)(2,1)}, bf16[64,4096]{1,0:T(8,128)(2,1)S(1)}, u32[]{:S(2)}, u32[]{:S(2)}) collective-permute-start(bf16[64,4096]{1,0:T(8,128)(2,1)} %collective-permute-done.1.refs_4_), channel_id=1, source_target_pairs={{0,112},{8,120},{16,0},{24,8},{32,16},{40,24},{48,32},{56,40},{64,... | collective-permute-start | bytes 1572872 | tf_op jit(solution)/shard_map/ppermute | solution.py:51
  26.5 0.8 copy-done.9
  27.3 2.9 %collective-permute-start.6 = (bf16[64,4096]{1,0:T(8,128)(2,1)}, bf16[64,4096]{1,0:T(8,128)(2,1)S(1)}, u32[]{:S(2)}, u32[]{:S(2)}) collective-permute-start(bf16[64,4096]{1,0:T(8,128)(2,1)} %collective-permute-done.1.refs_4_), channel_id=1, source_target_pairs={{0,128},{8,136},{16,144},{24,152},{32,160},{40,168},{48,176},{56,1... | collective-permute-start | bytes 1572872 | tf_op jit(solution)/shard_map/ppermute | solution.py:51
  30.2 5.3 %all-to-all-start = ((f32[16,64,128]{2,1,0:T(8,128)}), f32[16,64,128]{2,1,0:T(8,128)S(1)}, u32[]{:S(2)}, u32[]{:S(2)}) async-start(f32[16,64,128]{2,1,0:T(8,128)} %pack.1), calls=%async_computation | async-start | bytes 1048576 | tf_op jit(solution)/shard_map/all_to_all | solution.py:390
  35.7 2.9 %collective-permute-start.13 = (bf16[64,4096]{1,0:T(8,128)(2,1)}, bf16[64,4096]{1,0:T(8,128)(2,1)S(1)}, u32[]{:S(2)}, u32[]{:S(2)}) collective-permute-start(bf16[64,4096]{1,0:T(8,128)(2,1)} %collective-permute-done.refs_2_), channel_id=1, source_target_pairs={{0,128},{8,136},{16,144},{24,152},{32,160},{40,168},{48,176},{56,1... | collective-permute-start | bytes 1572872 | tf_op jit(solution)/shard_map/ppermute | solution.py:51
  38.5 6.3 %grad_columns.3.refs_8_ = bf16[448,2048]{1,0:T(8,128)(2,1)} custom-call(s32[5]{0:T(128)S(1)} %stack.88.place_ref, bf16[448,4096]{1,0:T(8,128)(2,1)} %weight_hbm.7, bf16[64,4096]{1,0:T(8,128)(2,1)} %bitcast.35, bf16[64,4096]{1,0:T(8,128)(2,1)} %copy-done.8, bf16[64,4096]{1,0:T(8,128)(2,1)} %collective-permute-done.refs_2_, ...), custom_call_target="tpu_custom_call" | custom-call | tf_op jit(solution)/shard_map/grad_columns/pallas_call | solution.py:57
  44.9 1.3 %collective-permute-start.11 = (bf16[64,4096]{1,0:T(8,128)(2,1)S(1)}, bf16[64,4096]{1,0:T(8,128)(2,1)}, u32[]{:S(2)}, u32[]{:S(2)}) collective-permute-start(bf16[64,4096]{1,0:T(8,128)(2,1)S(1)} %collective-permute-done.4.refs_0_), channel_id=1, source_target_pairs={{0,16},{8,24},{16,32},{24,40},{32,48},{40,56},{48,64},{56,72},{64,... | collective-permute-start | bytes 1572872 | tf_op jit(solution)/shard_map/ppermute | solution.py:51
  46.1 1.5 %collective-permute-start.12 = (bf16[64,4096]{1,0:T(8,128)(2,1)S(1)}, bf16[64,4096]{1,0:T(8,128)(2,1)}, u32[]{:S(2)}, u32[]{:S(2)}) collective-permute-start(bf16[64,4096]{1,0:T(8,128)(2,1)S(1)} %collective-permute-done.5.refs_2_), channel_id=1, source_target_pairs={{0,112},{8,120},{16,0},{24,8},{32,16},{40,24},{48,32},{56,40},{64,... | collective-permute-start | bytes 1572872 | tf_op jit(solution)/shard_map/ppermute | solution.py:51
  47.6 3.4 %all-to-all-done.packed_ref = f32[16,64,128]{2,1,0:T(8,128)S(1)} async-done(((f32[16,64,128]{2,1,0:T(8,128)}), f32[16,64,128]{2,1,0:T(8,128)S(1)}, u32[]{:S(2)}, u32[]{:S(2)}) %all-to-all-start) | async-done | bytes 524320 | tf_op jit(solution)/shard_map/all_to_all | solution.py:390
  51.1 0.6 left.1.left_ref
  51.7 4.8 %collective-permute-start.14 = (f32[32,128]{1,0:T(8,128)S(1)}, f32[32,128]{1,0:T(8,128)S(1)}, u32[]{:S(2)}, u32[]{:S(2)}) collective-permute-start(f32[32,128]{1,0:T(8,128)S(1)} %left.1.left_ref), channel_id=1, source_target_pairs={{0,8},{8,0},{16,24},{24,16},{32,40},{40,32},{48,56},{56,48},{64,72... | collective-permute-start | bytes 49160 | tf_op jit(solution)/shard_map/ppermute | solution.py:51
  57.6 1.6 %feats.1 = f32[16,8,128]{2,1,0:T(8,128)} custom-call(s32[3]{0:T(128)S(1)} %pad_add_fusion.info_ref, f32[16,64,128]{2,1,0:T(8,128)S(1)} %all-to-all-done.packed_ref, f32[32,128]{1,0:T(8,128)S(1)} %left.1.left_ref, f32[32,128]{1,0:T(8,128)S(1)} %collective-permute-done.14.other_ref, s32[1,2048]{1,0:T(1,128)S(1)} %copy-done), custom_call_target="tpu_custom_call" | custom-call | tf_op jit(solution)/shard_map/feats/pallas_call | solution.py:57
  59.2 1.0 collective-permute-start.20
  60.2 0.9 collective-permute-done.11.refs_6_
  61.1 1.4 %collective-permute-start.21 = (bf16[64,4096]{1,0:T(8,128)(2,1)}, bf16[64,4096]{1,0:T(8,128)(2,1)S(1)}, u32[]{:S(2)}, u32[]{:S(2)}) collective-permute-start(bf16[64,4096]{1,0:T(8,128)(2,1)} %collective-permute-done.11.refs_6_), channel_id=1, source_target_pairs={{0,8},{8,0},{16,24},{24,16},{32,40},{40,32},{48,56},{56,48},{64,72... | collective-permute-start | bytes 1572872 | tf_op jit(solution)/shard_map/ppermute | solution.py:51
  62.5 2.7 %collective-permute-start.17 = (bf16[64,4096]{1,0:T(8,128)(2,1)S(1)}, bf16[64,4096]{1,0:T(8,128)(2,1)}, u32[]{:S(2)}, u32[]{:S(2)}) collective-permute-start(bf16[64,4096]{1,0:T(8,128)(2,1)S(1)} %collective-permute-done.5.refs_2_), channel_id=1, source_target_pairs={{0,128},{8,136},{16,144},{24,152},{32,160},{40,168},{48,176},{56,1... | collective-permute-start | bytes 1572872 | tf_op jit(solution)/shard_map/ppermute | solution.py:51
  65.2 2.7 %collective-permute-start.16 = (bf16[64,4096]{1,0:T(8,128)(2,1)}, bf16[64,4096]{1,0:T(8,128)(2,1)}, u32[]{:S(2)}, u32[]{:S(2)}) collective-permute-start(bf16[64,4096]{1,0:T(8,128)(2,1)} %collective-permute-done.12.refs_0_), channel_id=1, source_target_pairs={{0,112},{8,120},{16,0},{24,8},{32,16},{40,24},{48,32},{56,40},{64,... | collective-permute-start | bytes 1572872 | tf_op jit(solution)/shard_map/ppermute | solution.py:51
  67.9 0.8 collective-permute-start.25
  68.8 0.8 copy-done.16
  69.5 0.8 collective-permute-start.26
  70.3 5.1 %all-to-all-start.1 = ((f32[16,8,128]{2,1,0:T(8,128)}), f32[16,8,128]{2,1,0:T(8,128)S(1)}, u32[]{:S(2)}, u32[]{:S(2)}) async-start(f32[16,8,128]{2,1,0:T(8,128)} %feats.1), calls=%async_computation.1 | async-start | bytes 131072 | tf_op jit(solution)/shard_map/all_to_all | solution.py:413
  75.6 6.3 %grad_columns.4.refs_8_ = bf16[448,2048]{1,0:T(8,128)(2,1)} custom-call(s32[5]{0:T(128)S(1)} %stack.93.place_ref, bf16[448,4096]{1,0:T(8,128)(2,1)} %weight_hbm.7, bf16[64,4096]{1,0:T(8,128)(2,1)} %copy-done.3, bf16[64,4096]{1,0:T(8,128)(2,1)} %copy-done.13, bf16[64,4096]{1,0:T(8,128)(2,1)} %copy-done.2, ...), custom_call_target="tpu_custom_call", output_to_operand_aliasing={{}: (10, {})} | custom-call | tf_op jit(solution)/shard_map/grad_columns/pallas_call | solution.py:57
  81.9 2.5 %all-to-all-done.1 = f32[16,8,128]{2,1,0:T(8,128)S(1)} async-done(((f32[16,8,128]{2,1,0:T(8,128)}), f32[16,8,128]{2,1,0:T(8,128)S(1)}, u32[]{:S(2)}, u32[]{:S(2)}) %all-to-all-start.1) | async-done | bytes 65568 | tf_op jit(solution)/shard_map/all_to_all | solution.py:413
  84.5 1.3 %collective-permute-start.27 = (bf16[64,4096]{1,0:T(8,128)(2,1)}, bf16[64,4096]{1,0:T(8,128)(2,1)}, u32[]{:S(2)}, u32[]{:S(2)}) collective-permute-start(bf16[64,4096]{1,0:T(8,128)(2,1)} %collective-permute-done.15.refs_4_), channel_id=1, source_target_pairs={{0,8},{8,0},{16,24},{24,16},{32,40},{40,32},{48,56},{56,48},{64,72... | collective-permute-start | bytes 1572872 | tf_op jit(solution)/shard_map/ppermute | solution.py:51
  85.9 0.7 collective-permute-start.22
  86.6 2.0 %collective-permute-start.23 = (bf16[64,4096]{1,0:T(8,128)(2,1)}, bf16[64,4096]{1,0:T(8,128)(2,1)S(1)}, u32[]{:S(2)}, u32[]{:S(2)}) collective-permute-start(bf16[64,4096]{1,0:T(8,128)(2,1)} %collective-permute-done.17.refs_0_), channel_id=1, source_target_pairs={{0,112},{8,120},{16,0},{24,8},{32,16},{40,24},{48,32},{56,40},{64,... | collective-permute-start | bytes 1572872 | tf_op jit(solution)/shard_map/ppermute | solution.py:51
  88.6 1.6 %collective-permute-start.24 = (bf16[64,4096]{1,0:T(8,128)(2,1)}, bf16[64,4096]{1,0:T(8,128)(2,1)S(1)}, u32[]{:S(2)}, u32[]{:S(2)}) collective-permute-start(bf16[64,4096]{1,0:T(8,128)(2,1)} %collective-permute-done.16.refs_6_), channel_id=1, source_target_pairs={{0,128},{8,136},{16,144},{24,152},{32,160},{40,168},{48,176},{56,1... | collective-permute-start | bytes 1572872 | tf_op jit(solution)/shard_map/ppermute | solution.py:51
  90.2 0.8 broadcast_in_dim.11
  91.0 4.1 %all-to-all-start.2 = ((f32[8,128,128]{2,1,0:T(8,128)}), f32[8,128,128]{2,1,0:T(8,128)S(1)}, u32[]{:S(2)}, u32[]{:S(2)}) async-start(f32[8,128,128]{2,1,0:T(8,128)} %broadcast_in_dim.11), calls=%async_computation.2 | async-start | bytes 1048576 | tf_op jit(solution)/shard_map/all_to_all | solution.py:422
  95.2 1.6 %collective-permute-start.30 = (bf16[64,4096]{1,0:T(8,128)(2,1)}, bf16[64,4096]{1,0:T(8,128)(2,1)S(1)}, u32[]{:S(2)}, u32[]{:S(2)}) collective-permute-start(bf16[64,4096]{1,0:T(8,128)(2,1)} %collective-permute-done.17.refs_0_), channel_id=1, source_target_pairs={{0,8},{8,0},{16,24},{24,16},{32,40},{40,32},{48,56},{56,48},{64,72... | collective-permute-start | bytes 1572872 | tf_op jit(solution)/shard_map/ppermute | solution.py:51
  96.8 6.3 %grad_columns.5.refs_8_ = bf16[448,2048]{1,0:T(8,128)(2,1)} custom-call(s32[5]{0:T(128)S(1)} %stack.98.place_ref, bf16[448,4096]{1,0:T(8,128)(2,1)} %weight_hbm.7, bf16[64,4096]{1,0:T(8,128)(2,1)} %collective-permute-done.12.refs_0_, bf16[64,4096]{1,0:T(8,128)(2,1)} %copy-done.7, bf16[64,4096]{1,0:T(8,128)(2,1)} %copy-done.5, ...), custom_call_target="tpu_custom_call", output_to_operand_aliasing={{}: (10, {})} | custom-call | tf_op jit(solution)/shard_map/grad_columns/pallas_call | solution.py:57
  103.0 4.3 %all-to-all-done.2.mine_ref = f32[8,128,128]{2,1,0:T(8,128)S(1)} async-done(((f32[8,128,128]{2,1,0:T(8,128)}), f32[8,128,128]{2,1,0:T(8,128)S(1)}, u32[]{:S(2)}, u32[]{:S(2)}) %all-to-all-start.2) | async-done | bytes 524320 | tf_op jit(solution)/shard_map/all_to_all | solution.py:422
  107.4 2.1 %collective-permute-start.29 = (f32[8,128,128]{2,1,0:T(8,128)S(1)}, f32[8,128,128]{2,1,0:T(8,128)S(1)}, u32[]{:S(2)}, u32[]{:S(2)}) collective-permute-start(f32[8,128,128]{2,1,0:T(8,128)S(1)} %all-to-all-done.2.mine_ref), channel_id=1, source_target_pairs={{0,8},{8,0},{16,24},{24,16},{32,40},{40,32},{48,56},{56,48},{64,72... | collective-permute-start | bytes 1572872 | tf_op jit(solution)/shard_map/ppermute | solution.py:51
  110.3 0.8 collective-permute-done.29.other_ref
  111.1 0.9 collective-permute-done.31.refs_3_
  112.0 0.7 collective-permute-done.32.refs_5_
  112.7 0.7 collective-permute-done.33.refs_7_
  113.5 10.2 %finish.1 = (bf16[448,2048]{1,0:T(8,128)(2,1)}, f32[512,128]{1,0:T(8,128)}, f32[1,64]{1,0:T(1,128)}) custom-call(s32[3]{0:T(128)S(1)} %pad_add_fusion.info_ref, s32[4]{0:T(128)S(1)} %pad_add_fusion.1.place_ref, f32[8,128,128]{2,1,0:T(8,128)S(1)} %all-to-all-done.2.mine_ref, ...), custom_call_target="tpu_custom_call", output_to_operand_aliasing={{0}: (13, {})} | custom-call | tf_op jit(solution)/shard_map/finish/pallas_call | solution.py:57
  (76 shorter events, 3.1 us)
Async XLA Ops:
  0.6 14.0 %copy-start.1 = (bf16[1,64,4096]{2,1,0:T(8,128)(2,1)S(1)}, bf16[1,64,4096]{2,1,0:T(8,128)(2,1)}, u32[]{:S(2)}) copy-start(bf16[1,64,4096]{2,1,0:T(8,128)(2,1)} %param.7) | copy-start | bytes 1572868
  0.6 18.5 %collective-permute-start = (bf16[64,4096]{1,0:T(8,128)(2,1)}, bf16[64,4096]{1,0:T(8,128)(2,1)}, u32[]{:S(2)}, u32[]{:S(2)}) collective-permute-start(bf16[64,4096]{1,0:T(8,128)(2,1)} %bitcast.31), channel_id=1, source_target_pairs={{0,16},{8,24},{16,32},{24,40},{32,48},{40,56},{48,64},{56,72},{64,... | collective-permute-start | bytes 1572872 | tf_op jit(solution)/shard_map/ppermute | solution.py:51
  3.2 15.9 %collective-permute-start.1 = (bf16[64,4096]{1,0:T(8,128)(2,1)}, bf16[64,4096]{1,0:T(8,128)(2,1)}, u32[]{:S(2)}, u32[]{:S(2)}) collective-permute-start(bf16[64,4096]{1,0:T(8,128)(2,1)} %bitcast.32), channel_id=1, source_target_pairs={{0,112},{8,120},{16,0},{24,8},{32,16},{40,24},{48,32},{56,40},{64,... | collective-permute-start | bytes 1572872 | tf_op jit(solution)/shard_map/ppermute | solution.py:51
  7.2 14.2 %collective-permute-start.2 = (bf16[64,4096]{1,0:T(8,128)(2,1)}, bf16[64,4096]{1,0:T(8,128)(2,1)S(1)}, u32[]{:S(2)}, u32[]{:S(2)}) collective-permute-start(bf16[64,4096]{1,0:T(8,128)(2,1)} %bitcast.33), channel_id=1, source_target_pairs={{0,128},{8,136},{16,144},{24,152},{32,160},{40,168},{48,176},{56,1... | collective-permute-start | bytes 1572872 | tf_op jit(solution)/shard_map/ppermute | solution.py:51
  13.3 2.5 %collective-permute-start.3 = (f32[32,2176]{1,0:T(8,128)S(1)}, f32[32,2176]{1,0:T(8,128)S(1)}, u32[]{:S(2)}, u32[]{:S(2)}) collective-permute-start(f32[32,2176]{1,0:T(8,128)S(1)} %get-tuple-element.31), channel_id=1, source_target_pairs={{0,8},{8,0},{16,24},{24,16},{32,40},{40,32},{48,56},{56,48},{64,72... | collective-permute-start | bytes 835592 | tf_op jit(solution)/shard_map/ppermute | solution.py:51
  14.6 9.2 %collective-permute-start.7 = (bf16[64,4096]{1,0:T(8,128)(2,1)S(1)}, bf16[64,4096]{1,0:T(8,128)(2,1)S(1)}, u32[]{:S(2)}, u32[]{:S(2)}) collective-permute-start(bf16[64,4096]{1,0:T(8,128)(2,1)S(1)} %bitcast.36), channel_id=1, source_target_pairs={{0,8},{8,0},{16,24},{24,16},{32,40},{40,32},{48,56},{56,48},{64,72... | collective-permute-start | bytes 1572872 | tf_op jit(solution)/shard_map/ppermute | solution.py:51
  21.4 8.7 %copy-start.6 = (bf16[64,4096]{1,0:T(8,128)(2,1)}, bf16[64,4096]{1,0:T(8,128)(2,1)S(1)}, u32[]{:S(2)}) copy-start(bf16[64,4096]{1,0:T(8,128)(2,1)S(1)} %collective-permute-done.2.refs_6_) | copy-start | bytes 1572868
  21.4 5.0 %collective-permute-start.10 = (bf16[64,4096]{1,0:T(8,128)(2,1)S(1)}, bf16[64,4096]{1,0:T(8,128)(2,1)S(1)}, u32[]{:S(2)}, u32[]{:S(2)}) collective-permute-start(bf16[64,4096]{1,0:T(8,128)(2,1)S(1)} %collective-permute-done.2.refs_6_), channel_id=1, source_target_pairs={{0,8},{8,0},{16,24},{24,16},{32,40},{40,32},{48,56},{56,48},{64,72... | collective-permute-start | bytes 1572872 | tf_op jit(solution)/shard_map/ppermute | solution.py:51
  23.3 12.4 %collective-permute-start.8 = (bf16[64,4096]{1,0:T(8,128)(2,1)}, bf16[64,4096]{1,0:T(8,128)(2,1)}, u32[]{:S(2)}, u32[]{:S(2)}) collective-permute-start(bf16[64,4096]{1,0:T(8,128)(2,1)} %collective-permute-done.refs_2_), channel_id=1, source_target_pairs={{0,8},{8,0},{16,24},{24,16},{32,40},{40,32},{48,56},{56,48},{64,72... | collective-permute-start | bytes 1572872 | tf_op jit(solution)/shard_map/ppermute | solution.py:51
  23.3 15.3 %collective-permute-start.9 = (bf16[64,4096]{1,0:T(8,128)(2,1)}, bf16[64,4096]{1,0:T(8,128)(2,1)}, u32[]{:S(2)}, u32[]{:S(2)}) collective-permute-start(bf16[64,4096]{1,0:T(8,128)(2,1)} %collective-permute-done.1.refs_4_), channel_id=1, source_target_pairs={{0,8},{8,0},{16,24},{24,16},{32,40},{40,32},{48,56},{56,48},{64,72... | collective-permute-start | bytes 1572872 | tf_op jit(solution)/shard_map/ppermute | solution.py:51
  23.8 21.0 %collective-permute-start.4 = (bf16[64,4096]{1,0:T(8,128)(2,1)}, bf16[64,4096]{1,0:T(8,128)(2,1)S(1)}, u32[]{:S(2)}, u32[]{:S(2)}) collective-permute-start(bf16[64,4096]{1,0:T(8,128)(2,1)} %collective-permute-done.refs_2_), channel_id=1, source_target_pairs={{0,16},{8,24},{16,32},{24,40},{32,48},{40,56},{48,64},{56,72},{64,... | collective-permute-start | bytes 1572872 | tf_op jit(solution)/shard_map/ppermute | solution.py:51
  23.8 11.8 %copy-start.8 = (bf16[64,4096]{1,0:T(8,128)(2,1)}, bf16[64,4096]{1,0:T(8,128)(2,1)S(1)}, u32[]{:S(2)}) copy-start(bf16[64,4096]{1,0:T(8,128)(2,1)S(1)} %collective-permute-done.7.refs_1_) | copy-start | bytes 1572868
  23.8 21.0 %collective-permute-start.5 = (bf16[64,4096]{1,0:T(8,128)(2,1)}, bf16[64,4096]{1,0:T(8,128)(2,1)S(1)}, u32[]{:S(2)}, u32[]{:S(2)}) collective-permute-start(bf16[64,4096]{1,0:T(8,128)(2,1)} %collective-permute-done.1.refs_4_), channel_id=1, source_target_pairs={{0,112},{8,120},{16,0},{24,8},{32,16},{40,24},{48,32},{56,40},{64,... | collective-permute-start | bytes 1572872 | tf_op jit(solution)/shard_map/ppermute | solution.py:51
  27.3 17.6 %collective-permute-start.6 = (bf16[64,4096]{1,0:T(8,128)(2,1)}, bf16[64,4096]{1,0:T(8,128)(2,1)S(1)}, u32[]{:S(2)}, u32[]{:S(2)}) collective-permute-start(bf16[64,4096]{1,0:T(8,128)(2,1)} %collective-permute-done.1.refs_4_), channel_id=1, source_target_pairs={{0,128},{8,136},{16,144},{24,152},{32,160},{40,168},{48,176},{56,1... | collective-permute-start | bytes 1572872 | tf_op jit(solution)/shard_map/ppermute | solution.py:51
  30.2 20.9 %all-to-all-start = ((f32[16,64,128]{2,1,0:T(8,128)}), f32[16,64,128]{2,1,0:T(8,128)S(1)}, u32[]{:S(2)}, u32[]{:S(2)}) async-start(f32[16,64,128]{2,1,0:T(8,128)} %pack.1), calls=%async_computation | async-start | bytes 1048576 | tf_op jit(solution)/shard_map/all_to_all | solution.py:390
  35.7 21.9 %copy-start = (s32[1,2048]{1,0:T(1,128)S(1)}, s32[1,2048]{1,0:T(1,128)}, u32[]{:S(2)}) copy-start(s32[1,2048]{1,0:T(1,128)} %ids_ref.1) | copy-start | bytes 24580
  35.7 23.5 %collective-permute-start.13 = (bf16[64,4096]{1,0:T(8,128)(2,1)}, bf16[64,4096]{1,0:T(8,128)(2,1)S(1)}, u32[]{:S(2)}, u32[]{:S(2)}) collective-permute-start(bf16[64,4096]{1,0:T(8,128)(2,1)} %collective-permute-done.refs_2_), channel_id=1, source_target_pairs={{0,128},{8,136},{16,144},{24,152},{32,160},{40,168},{48,176},{56,1... | collective-permute-start | bytes 1572872 | tf_op jit(solution)/shard_map/ppermute | solution.py:51
  44.8 30.8 %copy-start.3 = (bf16[64,4096]{1,0:T(8,128)(2,1)}, bf16[64,4096]{1,0:T(8,128)(2,1)S(1)}, u32[]{:S(2)}) copy-start(bf16[64,4096]{1,0:T(8,128)(2,1)S(1)} %collective-permute-done.4.refs_0_) | copy-start | bytes 1572868
  44.9 30.8 %copy-start.2 = (bf16[64,4096]{1,0:T(8,128)(2,1)}, bf16[64,4096]{1,0:T(8,128)(2,1)S(1)}, u32[]{:S(2)}) copy-start(bf16[64,4096]{1,0:T(8,128)(2,1)S(1)} %collective-permute-done.5.refs_2_) | copy-start | bytes 1572868
  44.9 30.7 %copy-start.4 = (bf16[64,4096]{1,0:T(8,128)(2,1)}, bf16[64,4096]{1,0:T(8,128)(2,1)S(1)}, u32[]{:S(2)}) copy-start(bf16[64,4096]{1,0:T(8,128)(2,1)S(1)} %collective-permute-done.6.refs_4_) | copy-start | bytes 1572868
  44.9 16.2 %collective-permute-start.11 = (bf16[64,4096]{1,0:T(8,128)(2,1)S(1)}, bf16[64,4096]{1,0:T(8,128)(2,1)}, u32[]{:S(2)}, u32[]{:S(2)}) collective-permute-start(bf16[64,4096]{1,0:T(8,128)(2,1)S(1)} %collective-permute-done.4.refs_0_), channel_id=1, source_target_pairs={{0,16},{8,24},{16,32},{24,40},{32,48},{40,56},{48,64},{56,72},{64,... | collective-permute-start | bytes 1572872 | tf_op jit(solution)/shard_map/ppermute | solution.py:51
  46.1 14.9 %collective-permute-start.12 = (bf16[64,4096]{1,0:T(8,128)(2,1)S(1)}, bf16[64,4096]{1,0:T(8,128)(2,1)}, u32[]{:S(2)}, u32[]{:S(2)}) collective-permute-start(bf16[64,4096]{1,0:T(8,128)(2,1)S(1)} %collective-permute-done.5.refs_2_), channel_id=1, source_target_pairs={{0,112},{8,120},{16,0},{24,8},{32,16},{40,24},{48,32},{56,40},{64,... | collective-permute-start | bytes 1572872 | tf_op jit(solution)/shard_map/ppermute | solution.py:51
  51.7 5.6 %collective-permute-start.14 = (f32[32,128]{1,0:T(8,128)S(1)}, f32[32,128]{1,0:T(8,128)S(1)}, u32[]{:S(2)}, u32[]{:S(2)}) collective-permute-start(f32[32,128]{1,0:T(8,128)S(1)} %left.1.left_ref), channel_id=1, source_target_pairs={{0,8},{8,0},{16,24},{24,16},{32,40},{40,32},{48,56},{56,48},{64,72... | collective-permute-start | bytes 49160 | tf_op jit(solution)/shard_map/ppermute | solution.py:51
  56.4 8.8 %collective-permute-start.18 = (bf16[64,4096]{1,0:T(8,128)(2,1)S(1)}, bf16[64,4096]{1,0:T(8,128)(2,1)S(1)}, u32[]{:S(2)}, u32[]{:S(2)}) collective-permute-start(bf16[64,4096]{1,0:T(8,128)(2,1)S(1)} %collective-permute-done.4.refs_0_), channel_id=1, source_target_pairs={{0,8},{8,0},{16,24},{24,16},{32,40},{40,32},{48,56},{56,48},{64,72... | collective-permute-start | bytes 1572872 | tf_op jit(solution)/shard_map/ppermute | solution.py:51
  57.2 8.0 %collective-permute-start.19 = (bf16[64,4096]{1,0:T(8,128)(2,1)S(1)}, bf16[64,4096]{1,0:T(8,128)(2,1)S(1)}, u32[]{:S(2)}, u32[]{:S(2)}) collective-permute-start(bf16[64,4096]{1,0:T(8,128)(2,1)S(1)} %collective-permute-done.5.refs_2_), channel_id=1, source_target_pairs={{0,8},{8,0},{16,24},{24,16},{32,40},{40,32},{48,56},{56,48},{64,72... | collective-permute-start | bytes 1572872 | tf_op jit(solution)/shard_map/ppermute | solution.py:51
  59.2 22.7 %copy-start.5 = (bf16[64,4096]{1,0:T(8,128)(2,1)}, bf16[64,4096]{1,0:T(8,128)(2,1)S(1)}, u32[]{:S(2)}) copy-start(bf16[64,4096]{1,0:T(8,128)(2,1)S(1)} %collective-permute-done.13.refs_2_) | copy-start | bytes 1572868
  59.2 8.7 %collective-permute-start.20 = (bf16[64,4096]{1,0:T(8,128)(2,1)S(1)}, bf16[64,4096]{1,0:T(8,128)(2,1)S(1)}, u32[]{:S(2)}, u32[]{:S(2)}) collective-permute-start(bf16[64,4096]{1,0:T(8,128)(2,1)S(1)} %collective-permute-done.6.refs_4_), channel_id=1, source_target_pairs={{0,8},{8,0},{16,24},{24,16},{32,40},{40,32},{48,56},{56,48},{64,72... | collective-permute-start | bytes 1572872 | tf_op jit(solution)/shard_map/ppermute | solution.py:51
  61.1 7.6 %collective-permute-start.21 = (bf16[64,4096]{1,0:T(8,128)(2,1)}, bf16[64,4096]{1,0:T(8,128)(2,1)S(1)}, u32[]{:S(2)}, u32[]{:S(2)}) collective-permute-start(bf16[64,4096]{1,0:T(8,128)(2,1)} %collective-permute-done.11.refs_6_), channel_id=1, source_target_pairs={{0,8},{8,0},{16,24},{24,16},{32,40},{40,32},{48,56},{56,48},{64,72... | collective-permute-start | bytes 1572872 | tf_op jit(solution)/shard_map/ppermute | solution.py:51
  62.5 19.4 %collective-permute-start.17 = (bf16[64,4096]{1,0:T(8,128)(2,1)S(1)}, bf16[64,4096]{1,0:T(8,128)(2,1)}, u32[]{:S(2)}, u32[]{:S(2)}) collective-permute-start(bf16[64,4096]{1,0:T(8,128)(2,1)S(1)} %collective-permute-done.5.refs_2_), channel_id=1, source_target_pairs={{0,128},{8,136},{16,144},{24,152},{32,160},{40,168},{48,176},{56,1... | collective-permute-start | bytes 1572872 | tf_op jit(solution)/shard_map/ppermute | solution.py:51
  65.2 19.3 %collective-permute-start.15 = (bf16[64,4096]{1,0:T(8,128)(2,1)S(1)}, bf16[64,4096]{1,0:T(8,128)(2,1)}, u32[]{:S(2)}, u32[]{:S(2)}) collective-permute-start(bf16[64,4096]{1,0:T(8,128)(2,1)S(1)} %collective-permute-done.13.refs_2_), channel_id=1, source_target_pairs={{0,16},{8,24},{16,32},{24,40},{32,48},{40,56},{48,64},{56,72},{64,... | collective-permute-start | bytes 1572872 | tf_op jit(solution)/shard_map/ppermute | solution.py:51
  65.2 19.2 %collective-permute-start.16 = (bf16[64,4096]{1,0:T(8,128)(2,1)}, bf16[64,4096]{1,0:T(8,128)(2,1)}, u32[]{:S(2)}, u32[]{:S(2)}) collective-permute-start(bf16[64,4096]{1,0:T(8,128)(2,1)} %collective-permute-done.12.refs_0_), channel_id=1, source_target_pairs={{0,112},{8,120},{16,0},{24,8},{32,16},{40,24},{48,32},{56,40},{64,... | collective-permute-start | bytes 1572872 | tf_op jit(solution)/shard_map/ppermute | solution.py:51
  67.9 18.7 %collective-permute-start.25 = (bf16[64,4096]{1,0:T(8,128)(2,1)}, bf16[64,4096]{1,0:T(8,128)(2,1)S(1)}, u32[]{:S(2)}, u32[]{:S(2)}) collective-permute-start(bf16[64,4096]{1,0:T(8,128)(2,1)} %collective-permute-done.12.refs_0_), channel_id=1, source_target_pairs={{0,8},{8,0},{16,24},{24,16},{32,40},{40,32},{48,56},{56,48},{64,72... | collective-permute-start | bytes 1572872 | tf_op jit(solution)/shard_map/ppermute | solution.py:51
  69.5 19.0 %collective-permute-start.26 = (bf16[64,4096]{1,0:T(8,128)(2,1)S(1)}, bf16[64,4096]{1,0:T(8,128)(2,1)}, u32[]{:S(2)}, u32[]{:S(2)}) collective-permute-start(bf16[64,4096]{1,0:T(8,128)(2,1)S(1)} %collective-permute-done.13.refs_2_), channel_id=1, source_target_pairs={{0,8},{8,0},{16,24},{24,16},{32,40},{40,32},{48,56},{56,48},{64,72... | collective-permute-start | bytes 1572872 | tf_op jit(solution)/shard_map/ppermute | solution.py:51
  70.3 14.1 %all-to-all-start.1 = ((f32[16,8,128]{2,1,0:T(8,128)}), f32[16,8,128]{2,1,0:T(8,128)S(1)}, u32[]{:S(2)}, u32[]{:S(2)}) async-start(f32[16,8,128]{2,1,0:T(8,128)} %feats.1), calls=%async_computation.1 | async-start | bytes 131072 | tf_op jit(solution)/shard_map/all_to_all | solution.py:413
  84.5 10.8 %collective-permute-start.27 = (bf16[64,4096]{1,0:T(8,128)(2,1)}, bf16[64,4096]{1,0:T(8,128)(2,1)}, u32[]{:S(2)}, u32[]{:S(2)}) collective-permute-start(bf16[64,4096]{1,0:T(8,128)(2,1)} %collective-permute-done.15.refs_4_), channel_id=1, source_target_pairs={{0,8},{8,0},{16,24},{24,16},{32,40},{40,32},{48,56},{56,48},{64,72... | collective-permute-start | bytes 1572872 | tf_op jit(solution)/shard_map/ppermute | solution.py:51
  85.8 11.0 %collective-permute-start.28 = (bf16[64,4096]{1,0:T(8,128)(2,1)}, bf16[64,4096]{1,0:T(8,128)(2,1)}, u32[]{:S(2)}, u32[]{:S(2)}) collective-permute-start(bf16[64,4096]{1,0:T(8,128)(2,1)} %collective-permute-done.16.refs_6_), channel_id=1, source_target_pairs={{0,8},{8,0},{16,24},{24,16},{32,40},{40,32},{48,56},{56,48},{64,72... | collective-permute-start | bytes 1572872 | tf_op jit(solution)/shard_map/ppermute | solution.py:51
  85.9 21.5 %collective-permute-start.22 = (bf16[64,4096]{1,0:T(8,128)(2,1)}, bf16[64,4096]{1,0:T(8,128)(2,1)S(1)}, u32[]{:S(2)}, u32[]{:S(2)}) collective-permute-start(bf16[64,4096]{1,0:T(8,128)(2,1)} %collective-permute-done.15.refs_4_), channel_id=1, source_target_pairs={{0,16},{8,24},{16,32},{24,40},{32,48},{40,56},{48,64},{56,72},{64,... | collective-permute-start | bytes 1572872 | tf_op jit(solution)/shard_map/ppermute | solution.py:51
  86.6 20.8 %collective-permute-start.23 = (bf16[64,4096]{1,0:T(8,128)(2,1)}, bf16[64,4096]{1,0:T(8,128)(2,1)S(1)}, u32[]{:S(2)}, u32[]{:S(2)}) collective-permute-start(bf16[64,4096]{1,0:T(8,128)(2,1)} %collective-permute-done.17.refs_0_), channel_id=1, source_target_pairs={{0,112},{8,120},{16,0},{24,8},{32,16},{40,24},{48,32},{56,40},{64,... | collective-permute-start | bytes 1572872 | tf_op jit(solution)/shard_map/ppermute | solution.py:51
  88.6 18.8 %collective-permute-start.24 = (bf16[64,4096]{1,0:T(8,128)(2,1)}, bf16[64,4096]{1,0:T(8,128)(2,1)S(1)}, u32[]{:S(2)}, u32[]{:S(2)}) collective-permute-start(bf16[64,4096]{1,0:T(8,128)(2,1)} %collective-permute-done.16.refs_6_), channel_id=1, source_target_pairs={{0,128},{8,136},{16,144},{24,152},{32,160},{40,168},{48,176},{56,1... | collective-permute-start | bytes 1572872 | tf_op jit(solution)/shard_map/ppermute | solution.py:51
  91.0 16.4 %all-to-all-start.2 = ((f32[8,128,128]{2,1,0:T(8,128)}), f32[8,128,128]{2,1,0:T(8,128)S(1)}, u32[]{:S(2)}, u32[]{:S(2)}) async-start(f32[8,128,128]{2,1,0:T(8,128)} %broadcast_in_dim.11), calls=%async_computation.2 | async-start | bytes 1048576 | tf_op jit(solution)/shard_map/all_to_all | solution.py:422
  95.2 15.1 %collective-permute-start.30 = (bf16[64,4096]{1,0:T(8,128)(2,1)}, bf16[64,4096]{1,0:T(8,128)(2,1)S(1)}, u32[]{:S(2)}, u32[]{:S(2)}) collective-permute-start(bf16[64,4096]{1,0:T(8,128)(2,1)} %collective-permute-done.17.refs_0_), channel_id=1, source_target_pairs={{0,8},{8,0},{16,24},{24,16},{32,40},{40,32},{48,56},{56,48},{64,72... | collective-permute-start | bytes 1572872 | tf_op jit(solution)/shard_map/ppermute | solution.py:51
  107.4 6.1 %copy-start.10 = (bf16[64,4096]{1,0:T(8,128)(2,1)}, bf16[64,4096]{1,0:T(8,128)(2,1)S(1)}, u32[]{:S(2)}) copy-start(bf16[64,4096]{1,0:T(8,128)(2,1)S(1)} %collective-permute-done.22.refs_2_) | copy-start | bytes 1572868
  107.4 6.1 %copy-start.11 = (bf16[64,4096]{1,0:T(8,128)(2,1)}, bf16[64,4096]{1,0:T(8,128)(2,1)S(1)}, u32[]{:S(2)}) copy-start(bf16[64,4096]{1,0:T(8,128)(2,1)S(1)} %collective-permute-done.23.refs_4_) | copy-start | bytes 1572868
  107.4 6.1 %copy-start.12 = (bf16[64,4096]{1,0:T(8,128)(2,1)}, bf16[64,4096]{1,0:T(8,128)(2,1)S(1)}, u32[]{:S(2)}) copy-start(bf16[64,4096]{1,0:T(8,128)(2,1)S(1)} %collective-permute-done.24.refs_6_) | copy-start | bytes 1572868
  107.4 3.7 %collective-permute-start.29 = (f32[8,128,128]{2,1,0:T(8,128)S(1)}, f32[8,128,128]{2,1,0:T(8,128)S(1)}, u32[]{:S(2)}, u32[]{:S(2)}) collective-permute-start(f32[8,128,128]{2,1,0:T(8,128)S(1)} %all-to-all-done.2.mine_ref), channel_id=1, source_target_pairs={{0,8},{8,0},{16,24},{24,16},{32,40},{40,32},{48,56},{56,48},{64,72... | collective-permute-start | bytes 1572872 | tf_op jit(solution)/shard_map/ppermute | solution.py:51
  109.5 2.4 %collective-permute-start.31 = (bf16[64,4096]{1,0:T(8,128)(2,1)S(1)}, bf16[64,4096]{1,0:T(8,128)(2,1)}, u32[]{:S(2)}, u32[]{:S(2)}) collective-permute-start(bf16[64,4096]{1,0:T(8,128)(2,1)S(1)} %collective-permute-done.22.refs_2_), channel_id=1, source_target_pairs={{0,8},{8,0},{16,24},{24,16},{32,40},{40,32},{48,56},{56,48},{64,72... | collective-permute-start | bytes 1572872 | tf_op jit(solution)/shard_map/ppermute | solution.py:51
  109.7 3.0 %collective-permute-start.32 = (bf16[64,4096]{1,0:T(8,128)(2,1)S(1)}, bf16[64,4096]{1,0:T(8,128)(2,1)}, u32[]{:S(2)}, u32[]{:S(2)}) collective-permute-start(bf16[64,4096]{1,0:T(8,128)(2,1)S(1)} %collective-permute-done.23.refs_4_), channel_id=1, source_target_pairs={{0,8},{8,0},{16,24},{24,16},{32,40},{40,32},{48,56},{56,48},{64,72... | collective-permute-start | bytes 1572872 | tf_op jit(solution)/shard_map/ppermute | solution.py:51
  110.1 3.4 %collective-permute-start.33 = (bf16[64,4096]{1,0:T(8,128)(2,1)S(1)}, bf16[64,4096]{1,0:T(8,128)(2,1)}, u32[]{:S(2)}, u32[]{:S(2)}) collective-permute-start(bf16[64,4096]{1,0:T(8,128)(2,1)S(1)} %collective-permute-done.24.refs_6_), channel_id=1, source_target_pairs={{0,8},{8,0},{16,24},{24,16},{32,40},{40,32},{48,56},{56,48},{64,72... | collective-permute-start | bytes 1572872 | tf_op jit(solution)/shard_map/ppermute | solution.py:51
  (7 other events, 17.1 us)
